TPU v7x, 256 devices: a whole 4x4x8 slice. The times are simulated.
256 devices in a mesh: grp: 8 (over y, core), dev: 32 (over x, z).
Axes of the slice: x: 4, y: 4, z: 8, core: 2. Of those that a mesh axis runs over, the one named last changes fastest.
Arguments:
- conc_old: float32 [256, 1024, 256], P('grp', 'dev'), may hold values from 0.5 to 2
- phi_old: float32 [256, 1024, 256], P('grp', 'dev'), may hold values from -6 to 6
- solid_pot: float32 [256, 1024, 256], P('grp', 'dev'), may hold values from -4.5 to 6
- phase_label: int32 [256, 1024, 256], P('grp', 'dev'), may hold values from 0 to 2
- iface_block: int32 [8, 8192], P('grp', 'dev'), may hold values from 0 to 2047
- iface_owner: int32 [8, 8192, 1], P('grp', 'dev'), may hold values from 0 to 31; in each aligned block of 256 rows (0 to 255, 256 to 511, ..., all dimensions but the last counted through in order) at most 16 rows name the same one
Outputs:
- concentration: float32 [256, 1024, 256], P('grp', 'dev')
- flux: float32 [256, 1024, 256], P('grp', 'dev')
- potential: float32 [256, 1024, 256], P('grp', 'dev')
Inputs may be any that keep to these rules, and one draw needn't show every extreme that they name: `iface_owner`: among the 256 entries of one index of dev, no owner is named more than 16 times, a bound that some block reaches.
All inputs are finite; a program needn't handle non-finite values.
Results may differ from a plain program's by a relative error of at most 0.0005.
Values sent between devices are 32-bit elements; how exact they have to be, the bound alone decides.
A program may use at most 64 MiB of HBM per device.

v0:
```python
import jax
import jax.numpy as jnp
from jax import lax
from jax.sharding import PartitionSpec as P

SWEEPS = 4
SMOOTH = 2
COARSE_SWEEPS = 8


MASS = 0.05
OMEGA = 0.8
DIFFUSION_TABLE = (1.5, 0.1, 0.4)
CONDUCT_TABLE = (1.0, 0.3, 0.6)
KINETIC_TABLE = (0.2, 1.0, 0.5)


def padded_2(value, sides, width):
    for axis, dim in sides:
        size, length = (lax.axis_size(axis), value.shape[dim])
        up = [(i, (i + 1) % size) for i in range(size - 1)]
        down = [(j, i) for i, j in up]
        last = lax.slice_in_dim(value, length - width, length, axis=dim)
        initial = lax.slice_in_dim(value, 0, width, axis=dim)
        before = lax.ppermute(last, axis, up)
        after = lax.ppermute(initial, axis, down)
        value = jnp.concatenate([before, value, after], axis=dim)
    return value


def lookup(phase_label, table_vals):
    return jnp.where(
        phase_label == 0, table_vals[0], jnp.where(phase_label == 1, table_vals[1], table_vals[2])
    ).astype(jnp.float32)


def split_parts(padded):
    middle = padded[1:-1, 1:-1, 1:-1]
    in_plane = (
        padded[2:, 1:-1, 1:-1]
        + padded[:-2, 1:-1, 1:-1]
        + padded[1:-1, 2:, 1:-1]
        + padded[1:-1, :-2, 1:-1]
    )
    along_z = padded[1:-1, 1:-1, 2:] + padded[1:-1, 1:-1, :-2]
    return (middle, in_plane, along_z)


def apply_level(padded, conduct, weight):
    middle, in_plane, along_z = split_parts(padded)
    return MASS * middle + conduct * (weight * (4.0 * middle - in_plane) + 2.0 * middle - along_z)


def zero_padded(field_in):
    return jnp.pad(field_in, 1)


def fine_padded(field_in):
    extended = padded_2(field_in, (("grp", 0), ("dev", 1)), 1)
    return jnp.pad(extended, ((0, 0), (0, 0), (1, 1)))


def level_padded(field_in):
    extended = padded_2(field_in, (("grp", 0), ("dev", 1)), 1)
    return jnp.pad(extended, ((0, 0), (0, 0), (1, 1)))


def smooth(current, source, conduct, weight, padder):
    diagonal = MASS + conduct * (4.0 * weight + 2.0)
    return current + OMEGA * (source - apply_level(padder(current), conduct, weight)) / diagonal


def residual_of(current, source, conduct, weight, padder):
    return source - apply_level(padder(current), conduct, weight)


def restrict(field_in):
    extent_x, extent_y, extent_z = field_in.shape
    return field_in.reshape(extent_x // 2, 2, extent_y // 2, 2, extent_z).mean(axis=(1, 3))


def inject(field_in):
    return jnp.repeat(jnp.repeat(field_in, 2, axis=0), 2, axis=1)


def butler_volmer(concentration, phi_old, solid_pot, kinetic):
    over_pot = solid_pot - phi_old - 0.2 * jnp.log(concentration)
    return 2.0 * kinetic * jnp.sqrt(concentration) * jnp.sinh(0.5 * over_pot)


def body(conc_old, phi_old, solid_pot, phase_label, iface_block, iface_owner):
    diffusion = lookup(phase_label, DIFFUSION_TABLE)
    concentration = conc_old
    for _ in range(SWEEPS):
        middle, in_plane, along_z = split_parts(fine_padded(concentration))
        concentration = (conc_old + diffusion * (in_plane + along_z)) / (1.0 + 6.0 * diffusion)
    kinetic = lookup(phase_label, KINETIC_TABLE)
    peer_count = lax.axis_size("dev")
    owners = iface_owner[0, :, 0]
    blocks = iface_block[0]
    capacity = 2 * owners.shape[0] // peer_count
    onehot = (owners[:, None] == jnp.arange(peer_count, dtype=jnp.int32)[None, :]).astype(jnp.int32)
    slot_rank = jnp.sum((jnp.cumsum(onehot, axis=0) - onehot) * onehot, axis=1)
    slot_pos = owners * capacity + slot_rank
    requests = (
        jnp.full((peer_count * capacity,), -1, jnp.int32)
        .at[slot_pos]
        .set(blocks)
        .reshape(peer_count, capacity)
    )
    requested = lax.all_to_all(requests, "dev", split_axis=0, concat_axis=0, tiled=True)
    block_count = concentration.size // 128
    targets = jnp.where(requested < 0, block_count, requested).reshape(-1)
    flux_all = butler_volmer(concentration, phi_old, solid_pot, kinetic).reshape(block_count, 128)
    listed = jnp.zeros((block_count,), jnp.float32).at[targets].set(1.0, mode="drop")
    flux = (flux_all * listed[:, None]).reshape(concentration.shape)
    conduct = lookup(phase_label, CONDUCT_TABLE) * conc_old
    source_fine = MASS * phi_old + flux
    potential = phi_old
    for _ in range(SMOOTH):
        potential = smooth(potential, source_fine, conduct, 1.0, fine_padded)
    resid_fine = residual_of(potential, source_fine, conduct, 1.0, fine_padded)
    conduct_mid = restrict(conduct)
    source_mid = restrict(resid_fine)
    error_mid = jnp.zeros_like(source_mid)
    for _ in range(SMOOTH):
        error_mid = smooth(error_mid, source_mid, conduct_mid, 0.25, level_padded)
    resid_mid = residual_of(error_mid, source_mid, conduct_mid, 0.25, level_padded)
    conduct_coarse = restrict(conduct_mid)
    source_coarse = restrict(resid_mid)
    source_slab, conduct_slab = (
        lax.all_gather(source_coarse, "dev", axis=1, tiled=True),
        lax.all_gather(conduct_coarse, "dev", axis=1, tiled=True),
    )
    error_slab = jnp.zeros_like(source_slab)
    for _ in range(COARSE_SWEEPS):
        error_slab = smooth(error_slab, source_slab, conduct_slab, 0.0625, zero_padded)
    resid_slab = residual_of(error_slab, source_slab, conduct_slab, 0.0625, zero_padded)
    load_slab = apply_level(zero_padded(jnp.ones_like(source_slab)), conduct_slab, 0.0625)
    error_slab = error_slab + jnp.sum(resid_slab) / jnp.sum(load_slab)
    width_local = source_coarse.shape[1]
    error_coarse = lax.dynamic_slice_in_dim(
        error_slab, lax.axis_index("dev") * width_local, width_local, 1
    )
    error_mid = error_mid + inject(error_coarse)
    for _ in range(SMOOTH):
        error_mid = smooth(error_mid, source_mid, conduct_mid, 0.25, level_padded)
    potential = potential + inject(error_mid)
    for _ in range(SMOOTH):
        potential = smooth(potential, source_fine, conduct, 1.0, fine_padded)
    return (concentration, flux, potential)


def solution(mesh):
    return jax.shard_map(
        body,
        mesh=mesh,
        in_specs=(
            P("grp", "dev", None),
            P("grp", "dev", None),
            P("grp", "dev", None),
            P("grp", "dev", None),
            P("grp", "dev"),
            P("grp", "dev", None),
        ),
        out_specs=(P("grp", "dev", None), P("grp", "dev", None), P("grp", "dev", None)),
        check_vma=False,
    )
```

profile of v0, /device:TPU:14, one launch (start us, length us, event | category | flops | bytes accessed | tf_op | source)
XLA Modules:
  0.0 485.7 jit_solution(3005724011805043479)
XLA Ops:
  9.9 3.6 collective-permute-start
  18.7 11.6 %all-to-all-start = ((s32[32,1,16]{2,1,0:T(1,128)}), s32[32,1,16]{2,1,0:T(1,128)S(1)}, u32[]{:S(2)}, u32[]{:S(2)}) async-start(s32[32,1,16]{2,1,0:T(1,128)} %bitcast.7), calls=%async_computation | async-start | bytes 32768 | tf_op jit(solution)/shard_map/all_to_all | solution.py:111
  31.8 5.0 %collective-permute-start.2 = (f32[34,1,256]{2,1,0:T(1,128)S(1)}, f32[34,1,256]{2,1,0:T(1,128)S(1)}, u32[]{:S(2)}, u32[]{:S(2)}) collective-permute-start(f32[34,1,256]{2,1,0:T(1,128)S(1)} %get-tuple-element.28), channel_id=1, source_target_pairs={{1,0},{2,1},{3,2},{4,3},{5,4},{6,5},{7,6},{8,7},{9,8},{10,9},{11,1... | collective-permute-start | bytes 104456 | tf_op jit(solution)/shard_map/ppermute | solution.py:26
  42.1 3.6 collective-permute-start.16
  48.0 3.2 fusion.218
  63.4 6.0 %collective-permute-start.6 = (f32[34,1,256]{2,1,0:T(1,128)S(1)}, f32[34,1,256]{2,1,0:T(1,128)S(1)}, u32[]{:S(2)}, u32[]{:S(2)}) collective-permute-start(f32[34,1,256]{2,1,0:T(1,128)S(1)} %get-tuple-element.26), channel_id=1, source_target_pairs={{1,0},{2,1},{3,2},{4,3},{5,4},{6,5},{7,6},{8,7},{9,8},{10,9},{11,1... | collective-permute-start | bytes 104456 | tf_op jit(solution)/shard_map/ppermute | solution.py:26
  72.1 5.6 %collective-permute-done.7 = f32[34,1,256]{2,1,0:T(1,128)S(1)} collective-permute-done((f32[34,1,256]{2,1,0:T(1,128)S(1)}, f32[34,1,256]{2,1,0:T(1,128)S(1)}, u32[]{:S(2)}, u32[]{:S(2)}) %collective-permute-start.7) | collective-permute-done | bytes 34848 | tf_op jit(solution)/shard_map/ppermute | solution.py:25
  88.9 4.1 collective-permute-start.11
  105.3 3.9 collective-permute-start.19
  109.3 4.0 collective-permute-start.14
  116.2 5.2 %collective-permute-done.15 = f32[34,1,256]{2,1,0:T(1,128)S(1)} collective-permute-done((f32[34,1,256]{2,1,0:T(1,128)S(1)}, f32[34,1,256]{2,1,0:T(1,128)S(1)}, u32[]{:S(2)}, u32[]{:S(2)}) %collective-permute-start.15) | collective-permute-done | bytes 34848 | tf_op jit(solution)/shard_map/ppermute | solution.py:25
  122.4 6.8 %fusion.188 = (f32[32,32,256]{2,1,0:T(8,128)S(1)}, f32[32,32,256]{2,1,0:T(8,128)S(1)}, f32[32,32,256]{2,1,0:T(8,128)S(1)}, f32[32,32,256]{2,1,0:T(8,128)}, f32[32,32,256]{2,1,0:T(8,128)}) fusion(f32[32,32,256]{2,1,0:T(8,128)S(1)} %copy-done.11, f32[34,34,258]{2,1,0:T(8,128)S(1)} %select_maximum_fusion.16, ...), kind=kLoop, calls=%fused_computation.323 | loop fusion | flops 17301504 | bytes 16588800 | tf_op jit(solution)/shard_map/add | solution.py:70
  138.3 3.9 collective-permute-start.23
  148.8 3.2 collective-permute-start.24
  154.0 4.0 collective-permute-start.30
  160.6 6.0 %collective-permute-start.26 = (f32[34,1,256]{2,1,0:T(1,128)}, f32[34,1,256]{2,1,0:T(1,128)S(1)}, u32[]{:S(2)}, u32[]{:S(2)}) collective-permute-start(f32[34,1,256]{2,1,0:T(1,128)} %get-tuple-element.18), channel_id=1, source_target_pairs={{1,0},{2,1},{3,2},{4,3},{5,4},{6,5},{7,6},{8,7},{9,8},{10,9},{11,1... | collective-permute-start | bytes 104456 | tf_op jit(solution)/shard_map/ppermute | solution.py:26
  189.6 5.8 %collective-permute-start.34 = (f32[18,1,256]{2,1,0:T(1,128)S(1)}, f32[18,1,256]{2,1,0:T(1,128)S(1)}, u32[]{:S(2)}, u32[]{:S(2)}) collective-permute-start(f32[18,1,256]{2,1,0:T(1,128)S(1)} %get-tuple-element.56), channel_id=1, source_target_pairs={{1,0},{2,1},{3,2},{4,3},{5,4},{6,5},{7,6},{8,7},{9,8},{10,9},{11,1... | collective-permute-start | bytes 55304 | tf_op jit(solution)/shard_map/ppermute | solution.py:26
  197.3 5.8 %collective-permute-done.35 = f32[18,1,256]{2,1,0:T(1,128)S(1)} collective-permute-done((f32[18,1,256]{2,1,0:T(1,128)S(1)}, f32[18,1,256]{2,1,0:T(1,128)S(1)}, u32[]{:S(2)}, u32[]{:S(2)}) %collective-permute-start.35) | collective-permute-done | bytes 18464 | tf_op jit(solution)/shard_map/ppermute | solution.py:25
  212.8 3.9 collective-permute-start.39
  216.7 3.8 collective-permute-done.39
  223.7 69.5 %all-gather.3.cloned.1.call-done = f32[8,256,256]{2,1,0:T(8,128)} async-done(((f32[8,8,256]{2,1,0:T(8,128)}), f32[8,256,256]{2,1,0:T(8,128)}) %all-gather.3.cloned.1.call-update) | async-done | bytes 2097168 | tf_op jit(solution)/shard_map/all_gather | solution.py:132
  293.2 76.6 %all-gather.5.cloned.1.call-done = f32[8,256,256]{2,1,0:T(8,128)} async-done(((f32[8,8,256]{2,1,0:T(8,128)}), f32[8,256,256]{2,1,0:T(8,128)}) %all-gather.5.cloned.1.call-update) | async-done | bytes 2097168 | tf_op jit(solution)/shard_map/all_gather | solution.py:133
  369.9 3.3 fusion.118
  389.9 4.2 fusion.130
  404.6 5.0 %collective-permute-start.42 = (f32[18,1,256]{2,1,0:T(1,128)S(1)}, f32[18,1,256]{2,1,0:T(1,128)S(1)}, u32[]{:S(2)}, u32[]{:S(2)}) collective-permute-start(f32[18,1,256]{2,1,0:T(1,128)S(1)} %get-tuple-element.52), channel_id=1, source_target_pairs={{1,0},{2,1},{3,2},{4,3},{5,4},{6,5},{7,6},{8,7},{9,8},{10,9},{11,1... | collective-permute-start | bytes 55304 | tf_op jit(solution)/shard_map/ppermute | solution.py:26
  411.7 5.7 %collective-permute-done.43 = f32[18,1,256]{2,1,0:T(1,128)S(1)} collective-permute-done((f32[18,1,256]{2,1,0:T(1,128)S(1)}, f32[18,1,256]{2,1,0:T(1,128)S(1)}, u32[]{:S(2)}, u32[]{:S(2)}) %collective-permute-start.43) | collective-permute-done | bytes 18464 | tf_op jit(solution)/shard_map/ppermute | solution.py:25
  427.1 3.9 collective-permute-start.47
  431.0 3.8 collective-permute-done.47
  448.4 3.9 collective-permute-start.51
  452.4 4.0 collective-permute-done.51
  467.7 3.9 collective-permute-start.55
  471.6 4.0 collective-permute-done.55
  (246 shorter events, 181.7 us)
Async XLA Ops:
  7.9 22.4 %collective-permute-start.1 = (f32[1,32,256]{2,1,0:T(8,128)S(1)}, f32[1,32,256]{2,1,0:T(8,128)S(1)}, u32[]{:S(2)}, u32[]{:S(2)}) collective-permute-start(f32[1,32,256]{2,1,0:T(8,128)S(1)} %get-tuple-element.46), channel_id=1, source_target_pairs={{0,32},{32,64},{64,96},{96,128},{128,160},{160,192},{192,224},{1,3... | collective-permute-start | bytes 98312 | tf_op jit(solution)/shard_map/ppermute | solution.py:25
  9.9 21.9 %collective-permute-start = (f32[1,32,256]{2,1,0:T(8,128)S(1)}, f32[1,32,256]{2,1,0:T(8,128)S(1)}, u32[]{:S(2)}, u32[]{:S(2)}) collective-permute-start(f32[1,32,256]{2,1,0:T(8,128)S(1)} %get-tuple-element.45), channel_id=1, source_target_pairs={{32,0},{64,32},{96,64},{128,96},{160,128},{192,160},{224,192},{33,... | collective-permute-start | bytes 98312 | tf_op jit(solution)/shard_map/ppermute | solution.py:26
  18.7 27.0 %all-to-all-start = ((s32[32,1,16]{2,1,0:T(1,128)}), s32[32,1,16]{2,1,0:T(1,128)S(1)}, u32[]{:S(2)}, u32[]{:S(2)}) async-start(s32[32,1,16]{2,1,0:T(1,128)} %bitcast.7), calls=%async_computation | async-start | bytes 32768 | tf_op jit(solution)/shard_map/all_to_all | solution.py:111
  30.3 262.9 %all-gather.3.cloned.1.call-start = ((), (), s32[]{:S(2)}) async-start(), calls=%async_computation.1 | async-start | bytes 2162688 | tf_op jit(solution)/shard_map/all_gather | solution.py:132
  31.8 15.2 %collective-permute-start.2 = (f32[34,1,256]{2,1,0:T(1,128)S(1)}, f32[34,1,256]{2,1,0:T(1,128)S(1)}, u32[]{:S(2)}, u32[]{:S(2)}) collective-permute-start(f32[34,1,256]{2,1,0:T(1,128)S(1)} %get-tuple-element.28), channel_id=1, source_target_pairs={{1,0},{2,1},{3,2},{4,3},{5,4},{6,5},{7,6},{8,7},{9,8},{10,9},{11,1... | collective-permute-start | bytes 104456 | tf_op jit(solution)/shard_map/ppermute | solution.py:26
  36.8 10.2 %collective-permute-start.3 = (f32[34,1,256]{2,1,0:T(1,128)S(1)}, f32[34,1,256]{2,1,0:T(1,128)S(1)}, u32[]{:S(2)}, u32[]{:S(2)}) collective-permute-start(f32[34,1,256]{2,1,0:T(1,128)S(1)} %get-tuple-element.27), channel_id=1, source_target_pairs={{0,1},{1,2},{2,3},{3,4},{4,5},{5,6},{6,7},{7,8},{8,9},{9,10},{10,1... | collective-permute-start | bytes 104456 | tf_op jit(solution)/shard_map/ppermute | solution.py:25
  40.2 31.2 %collective-permute-start.17 = (f32[1,32,256]{2,1,0:T(8,128)}, f32[1,32,256]{2,1,0:T(8,128)}, u32[]{:S(2)}, u32[]{:S(2)}) collective-permute-start(f32[1,32,256]{2,1,0:T(8,128)} %get-tuple-element.48), channel_id=1, source_target_pairs={{0,32},{32,64},{64,96},{96,128},{128,160},{160,192},{192,224},{1,3... | collective-permute-start | bytes 98312 | tf_op jit(solution)/shard_map/ppermute | solution.py:25
  42.1 51.0 %collective-permute-start.16 = (f32[1,32,256]{2,1,0:T(8,128)}, f32[1,32,256]{2,1,0:T(8,128)}, u32[]{:S(2)}, u32[]{:S(2)}) collective-permute-start(f32[1,32,256]{2,1,0:T(8,128)} %get-tuple-element.47), channel_id=1, source_target_pairs={{32,0},{64,32},{96,64},{128,96},{160,128},{192,160},{224,192},{33,... | collective-permute-start | bytes 98312 | tf_op jit(solution)/shard_map/ppermute | solution.py:26
  51.2 12.1 %collective-permute-start.4 = (f32[1,32,256]{2,1,0:T(8,128)S(1)}, f32[1,32,256]{2,1,0:T(8,128)S(1)}, u32[]{:S(2)}, u32[]{:S(2)}) collective-permute-start(f32[1,32,256]{2,1,0:T(8,128)S(1)} %get-tuple-element.44), channel_id=1, source_target_pairs={{32,0},{64,32},{96,64},{128,96},{160,128},{192,160},{224,192},{33,... | collective-permute-start | bytes 98312 | tf_op jit(solution)/shard_map/ppermute | solution.py:26
  53.1 10.2 %collective-permute-start.5 = (f32[1,32,256]{2,1,0:T(8,128)S(1)}, f32[1,32,256]{2,1,0:T(8,128)S(1)}, u32[]{:S(2)}, u32[]{:S(2)}) collective-permute-start(f32[1,32,256]{2,1,0:T(8,128)S(1)} %get-tuple-element.43), channel_id=1, source_target_pairs={{0,32},{32,64},{64,96},{96,128},{128,160},{160,192},{192,224},{1,3... | collective-permute-start | bytes 98312 | tf_op jit(solution)/shard_map/ppermute | solution.py:25
  63.4 8.7 %collective-permute-start.6 = (f32[34,1,256]{2,1,0:T(1,128)S(1)}, f32[34,1,256]{2,1,0:T(1,128)S(1)}, u32[]{:S(2)}, u32[]{:S(2)}) collective-permute-start(f32[34,1,256]{2,1,0:T(1,128)S(1)} %get-tuple-element.26), channel_id=1, source_target_pairs={{1,0},{2,1},{3,2},{4,3},{5,4},{6,5},{7,6},{8,7},{9,8},{10,9},{11,1... | collective-permute-start | bytes 104456 | tf_op jit(solution)/shard_map/ppermute | solution.py:26
  69.4 8.3 %collective-permute-start.7 = (f32[34,1,256]{2,1,0:T(1,128)S(1)}, f32[34,1,256]{2,1,0:T(1,128)S(1)}, u32[]{:S(2)}, u32[]{:S(2)}) collective-permute-start(f32[34,1,256]{2,1,0:T(1,128)S(1)} %get-tuple-element.25), channel_id=1, source_target_pairs={{0,1},{1,2},{2,3},{3,4},{4,5},{5,6},{6,7},{7,8},{8,9},{9,10},{10,1... | collective-permute-start | bytes 104456 | tf_op jit(solution)/shard_map/ppermute | solution.py:25
  88.9 7.9 %collective-permute-start.11 = (f32[34,1,256]{2,1,0:T(1,128)S(1)}, f32[34,1,256]{2,1,0:T(1,128)S(1)}, u32[]{:S(2)}, u32[]{:S(2)}) collective-permute-start(f32[34,1,256]{2,1,0:T(1,128)S(1)} %get-tuple-element.23), channel_id=1, source_target_pairs={{0,1},{1,2},{2,3},{3,4},{4,5},{5,6},{6,7},{7,8},{8,9},{9,10},{10,1... | collective-permute-start | bytes 104456 | tf_op jit(solution)/shard_map/ppermute | solution.py:25
  98.9 10.3 %collective-permute-start.12 = (f32[1,32,256]{2,1,0:T(8,128)S(1)}, f32[1,32,256]{2,1,0:T(8,128)S(1)}, u32[]{:S(2)}, u32[]{:S(2)}) collective-permute-start(f32[1,32,256]{2,1,0:T(8,128)S(1)} %get-tuple-element.40), channel_id=1, source_target_pairs={{32,0},{64,32},{96,64},{128,96},{160,128},{192,160},{224,192},{33,... | collective-permute-start | bytes 98312 | tf_op jit(solution)/shard_map/ppermute | solution.py:26
  100.9 8.3 %collective-permute-start.13 = (f32[1,32,256]{2,1,0:T(8,128)S(1)}, f32[1,32,256]{2,1,0:T(8,128)S(1)}, u32[]{:S(2)}, u32[]{:S(2)}) collective-permute-start(f32[1,32,256]{2,1,0:T(8,128)S(1)} %get-tuple-element.39), channel_id=1, source_target_pairs={{0,32},{32,64},{64,96},{96,128},{128,160},{160,192},{192,224},{1,3... | collective-permute-start | bytes 98312 | tf_op jit(solution)/shard_map/ppermute | solution.py:25
  103.3 11.9 %collective-permute-start.18 = (f32[34,1,256]{2,1,0:T(1,128)S(1)}, f32[34,1,256]{2,1,0:T(1,128)S(1)}, u32[]{:S(2)}, u32[]{:S(2)}) collective-permute-start(f32[34,1,256]{2,1,0:T(1,128)S(1)} %get-tuple-element.30), channel_id=1, source_target_pairs={{1,0},{2,1},{3,2},{4,3},{5,4},{6,5},{7,6},{8,7},{9,8},{10,9},{11,1... | collective-permute-start | bytes 104456 | tf_op jit(solution)/shard_map/ppermute | solution.py:26
  105.3 10.0 %collective-permute-start.19 = (f32[34,1,256]{2,1,0:T(1,128)S(1)}, f32[34,1,256]{2,1,0:T(1,128)S(1)}, u32[]{:S(2)}, u32[]{:S(2)}) collective-permute-start(f32[34,1,256]{2,1,0:T(1,128)S(1)} %get-tuple-element.29), channel_id=1, source_target_pairs={{0,1},{1,2},{2,3},{3,4},{4,5},{5,6},{6,7},{7,8},{8,9},{9,10},{10,1... | collective-permute-start | bytes 104456 | tf_op jit(solution)/shard_map/ppermute | solution.py:25
  113.3 8.1 %collective-permute-start.15 = (f32[34,1,256]{2,1,0:T(1,128)S(1)}, f32[34,1,256]{2,1,0:T(1,128)S(1)}, u32[]{:S(2)}, u32[]{:S(2)}) collective-permute-start(f32[34,1,256]{2,1,0:T(1,128)S(1)} %get-tuple-element.21), channel_id=1, source_target_pairs={{0,1},{1,2},{2,3},{3,4},{4,5},{5,6},{6,7},{7,8},{8,9},{9,10},{10,1... | collective-permute-start | bytes 104456 | tf_op jit(solution)/shard_map/ppermute | solution.py:25
  136.4 10.2 %collective-permute-start.22 = (f32[34,1,256]{2,1,0:T(1,128)S(1)}, f32[34,1,256]{2,1,0:T(1,128)S(1)}, u32[]{:S(2)}, u32[]{:S(2)}) collective-permute-start(f32[34,1,256]{2,1,0:T(1,128)S(1)} %get-tuple-element.20), channel_id=1, source_target_pairs={{1,0},{2,1},{3,2},{4,3},{5,4},{6,5},{7,6},{8,7},{9,8},{10,9},{11,1... | collective-permute-start | bytes 104456 | tf_op jit(solution)/shard_map/ppermute | solution.py:26
  138.3 8.3 %collective-permute-start.23 = (f32[34,1,256]{2,1,0:T(1,128)S(1)}, f32[34,1,256]{2,1,0:T(1,128)S(1)}, u32[]{:S(2)}, u32[]{:S(2)}) collective-permute-start(f32[34,1,256]{2,1,0:T(1,128)S(1)} %get-tuple-element.19), channel_id=1, source_target_pairs={{0,1},{1,2},{2,3},{3,4},{4,5},{5,6},{6,7},{7,8},{8,9},{9,10},{10,1... | collective-permute-start | bytes 104456 | tf_op jit(solution)/shard_map/ppermute | solution.py:25
  142.2 11.6 %collective-permute-start.28 = (f32[1,16,256]{2,1,0:T(8,128)S(1)}, f32[1,16,256]{2,1,0:T(8,128)S(1)}, u32[]{:S(2)}, u32[]{:S(2)}) collective-permute-start(f32[1,16,256]{2,1,0:T(8,128)S(1)} %broadcast.218), channel_id=1, source_target_pairs={{32,0},{64,32},{96,64},{128,96},{160,128},{192,160},{224,192},{33,... | collective-permute-start | bytes 49160 | tf_op jit(solution)/shard_map/ppermute | solution.py:26
  144.2 9.7 %collective-permute-start.29 = (f32[1,16,256]{2,1,0:T(8,128)S(1)}, f32[1,16,256]{2,1,0:T(8,128)S(1)}, u32[]{:S(2)}, u32[]{:S(2)}) collective-permute-start(f32[1,16,256]{2,1,0:T(8,128)S(1)} %broadcast.218), channel_id=1, source_target_pairs={{0,32},{32,64},{64,96},{96,128},{128,160},{160,192},{192,224},{1,3... | collective-permute-start | bytes 49160 | tf_op jit(solution)/shard_map/ppermute | solution.py:25
  148.8 11.2 %collective-permute-start.24 = (f32[1,32,256]{2,1,0:T(8,128)S(1)}, f32[1,32,256]{2,1,0:T(8,128)S(1)}, u32[]{:S(2)}, u32[]{:S(2)}) collective-permute-start(f32[1,32,256]{2,1,0:T(8,128)S(1)} %get-tuple-element.36), channel_id=1, source_target_pairs={{32,0},{64,32},{96,64},{128,96},{160,128},{192,160},{224,192},{33,... | collective-permute-start | bytes 98312 | tf_op jit(solution)/shard_map/ppermute | solution.py:26
  151.9 8.0 %collective-permute-start.25 = (f32[1,32,256]{2,1,0:T(8,128)S(1)}, f32[1,32,256]{2,1,0:T(8,128)S(1)}, u32[]{:S(2)}, u32[]{:S(2)}) collective-permute-start(f32[1,32,256]{2,1,0:T(8,128)S(1)} %get-tuple-element.35), channel_id=1, source_target_pairs={{0,32},{32,64},{64,96},{96,128},{128,160},{160,192},{192,224},{1,3... | collective-permute-start | bytes 98312 | tf_op jit(solution)/shard_map/ppermute | solution.py:25
  154.0 14.8 %collective-permute-start.30 = (f32[18,1,256]{2,1,0:T(1,128)S(1)}, f32[18,1,256]{2,1,0:T(1,128)S(1)}, u32[]{:S(2)}, u32[]{:S(2)}) collective-permute-start(f32[18,1,256]{2,1,0:T(1,128)S(1)} %get-tuple-element.58), channel_id=1, source_target_pairs={{1,0},{2,1},{3,2},{4,3},{5,4},{6,5},{7,6},{8,7},{9,8},{10,9},{11,1... | collective-permute-start | bytes 55304 | tf_op jit(solution)/shard_map/ppermute | solution.py:26
  158.0 10.8 %collective-permute-start.31 = (f32[18,1,256]{2,1,0:T(1,128)S(1)}, f32[18,1,256]{2,1,0:T(1,128)S(1)}, u32[]{:S(2)}, u32[]{:S(2)}) collective-permute-start(f32[18,1,256]{2,1,0:T(1,128)S(1)} %get-tuple-element.57), channel_id=1, source_target_pairs={{0,1},{1,2},{2,3},{3,4},{4,5},{5,6},{6,7},{7,8},{8,9},{9,10},{10,1... | collective-permute-start | bytes 55304 | tf_op jit(solution)/shard_map/ppermute | solution.py:25
  160.6 14.2 %collective-permute-start.26 = (f32[34,1,256]{2,1,0:T(1,128)}, f32[34,1,256]{2,1,0:T(1,128)S(1)}, u32[]{:S(2)}, u32[]{:S(2)}) collective-permute-start(f32[34,1,256]{2,1,0:T(1,128)} %get-tuple-element.18), channel_id=1, source_target_pairs={{1,0},{2,1},{3,2},{4,3},{5,4},{6,5},{7,6},{8,7},{9,8},{10,9},{11,1... | collective-permute-start | bytes 104456 | tf_op jit(solution)/shard_map/ppermute | solution.py:26
  166.7 8.4 %collective-permute-start.27 = (f32[34,1,256]{2,1,0:T(1,128)}, f32[34,1,256]{2,1,0:T(1,128)S(1)}, u32[]{:S(2)}, u32[]{:S(2)}) collective-permute-start(f32[34,1,256]{2,1,0:T(1,128)} %get-tuple-element.17), channel_id=1, source_target_pairs={{0,1},{1,2},{2,3},{3,4},{4,5},{5,6},{6,7},{7,8},{8,9},{9,10},{10,1... | collective-permute-start | bytes 104456 | tf_op jit(solution)/shard_map/ppermute | solution.py:25
  212.8 7.8 %collective-permute-start.39 = (f32[18,1,256]{2,1,0:T(1,128)S(1)}, f32[18,1,256]{2,1,0:T(1,128)S(1)}, u32[]{:S(2)}, u32[]{:S(2)}) collective-permute-start(f32[18,1,256]{2,1,0:T(1,128)S(1)} %get-tuple-element.53), channel_id=1, source_target_pairs={{0,1},{1,2},{2,3},{3,4},{4,5},{5,6},{6,7},{7,8},{8,9},{9,10},{10,1... | collective-permute-start | bytes 55304 | tf_op jit(solution)/shard_map/ppermute | solution.py:25
  222.2 147.5 %all-gather.5.cloned.1.call-start = ((), (), s32[]{:S(2)}) async-start(), calls=%async_computation.2 | async-start | bytes 2162688 | tf_op jit(solution)/shard_map/all_gather | solution.py:133
  448.4 7.9 %collective-permute-start.51 = (f32[34,1,256]{2,1,0:T(1,128)S(1)}, f32[34,1,256]{2,1,0:T(1,128)S(1)}, u32[]{:S(2)}, u32[]{:S(2)}) collective-permute-start(f32[34,1,256]{2,1,0:T(1,128)S(1)} %get-tuple-element.15), channel_id=1, source_target_pairs={{0,1},{1,2},{2,3},{3,4},{4,5},{5,6},{6,7},{7,8},{8,9},{9,10},{10,1... | collective-permute-start | bytes 104456 | tf_op jit(solution)/shard_map/ppermute | solution.py:25
  467.7 7.9 %collective-permute-start.55 = (f32[34,1,256]{2,1,0:T(1,128)S(1)}, f32[34,1,256]{2,1,0:T(1,128)S(1)}, u32[]{:S(2)}, u32[]{:S(2)}) collective-permute-start(f32[34,1,256]{2,1,0:T(1,128)S(1)} %get-tuple-element.13), channel_id=1, source_target_pairs={{0,1},{1,2},{2,3},{3,4},{4,5},{5,6},{6,7},{7,8},{8,9},{9,10},{10,1... | collective-permute-start | bytes 104456 | tf_op jit(solution)/shard_map/ppermute | solution.py:25
  (51 other events, 546.6 us)
Sparse Core Ops, SparseCore 0:
  222.4 70.7 all-gather.2
  295.7 74.0 all-gather.4
where the time goes:
time: 496 us; the launch traced here: 486 us
  waiting for transfers between devices  209 us (42%)
  starting transfers between devices  167 us (34%)
  other arithmetic  67.1 us (14%)
  local copies, waits for them, and re-layouts  25.2 us (5%)
  between operations  17 us (3%)
    ppermute x28, starting transfers between devices, padded_2(): after = lax.ppermute(initial, axis, down)  81.6 us
    all_gather x1, waiting for transfers between devices, body(): lax.all_gather(conduct_coarse, 'dev', axis=1, tiled=True)  76.6 us
    ppermute x28, starting transfers between devices, padded_2(): before = lax.ppermute(last, axis, up)  73.3 us
    all_gather x1, waiting for transfers between devices, body(): lax.all_gather(source_coarse, 'dev', axis=1, tiled=True)  69.5 us
    ppermute x28, waiting for transfers between devices, padded_2(): before = lax.ppermute(last, axis, up)  63.2 us
    add x14, other arithmetic, smooth(): current + OMEGA * (source - apply_level(padder(current), conduct, weight)...  28.6 us
    concatenate x26, other arithmetic, padded_2(): value = jnp.concatenate([before, value, after], axis=dim)  12.2 us
    all_to_all x1, starting transfers between devices, body(): lax.all_to_all(requests, 'dev', split_axis=0, concat_axis=0, tiled=True)  11.6 us
  transfers between devices with their start and end apart: 59, of which 20 were waited for; matrix products, arithmetic and copies ran while one was open for 7% of the time, Pallas kernels for 0%

commit v1 on v0

v1 whole, which is shorter than its diff:
```python
import functools

import jax
import jax.numpy as jnp
from jax import lax
from jax.experimental import pallas as pl
from jax.experimental.pallas import tpu as pltpu
from jax.sharding import PartitionSpec as P

MESH = pl.DeviceIdType.MESH
F32 = jnp.float32

FX, FY = 40, 48
MX, MY = 24, 32
EX, EY = 16, 24
GX, GY = 10, 40


def lookup(label, table):
    return jnp.where(label == 0, table[0], jnp.where(label == 1, table[1], table[2])).astype(F32)


def kernel(
    n_grp,
    n_dev,
    conc_hbm,
    phi_hbm,
    solid_hbm,
    label_hbm,
    lists_ref,
    conc_out,
    flux_out,
    pot_out,
    c0, lb, ph, sp, ca, cb, dd, cc, kk, gg, qq, bb, fx, p2,
    sm, km, gm, bm, m1, m2,
    kc, rc, gc, wa, wb, ka, kb, sc, ea, eb,
    ec,
    ysf, yrf, ysl, yrl, ysm, yrm, yse, yre,
    lrecv, msk, psend, precv,
    in_sem, out_sem, hs_sem, hr_sem, cs_sem, cr_sem, ls_sem, lr_sem, ps_sem, pr_sem,
):
    g = lax.axis_index("grp")
    d = lax.axis_index("dev")
    gu, gd = lax.rem(g + 1, n_grp), lax.rem(g + n_grp - 1, n_grp)
    du, dl = lax.rem(d + 1, n_dev), lax.rem(d + n_dev - 1, n_dev)
    eight = [(gd, dl), (gd, d), (gd, du), (g, dl), (g, du), (gu, dl), (gu, d), (gu, du)]
    lane = lax.broadcasted_iota(jnp.int32, (1, 128), 1)
    l0, l1 = lane == 0, lane == 127

    loads = []
    for k, (src, dst) in enumerate(((conc_hbm, c0), (label_hbm, lb), (phi_hbm, ph))):
        for h in range(2):
            loads.append(
                pltpu.make_async_copy(
                    src.at[:, :, pl.ds(128 * h, 128)], dst.at[pl.ds(4, 32), h, pl.ds(8, 32), :], in_sem.at[2 * k + h]
                )
            )
    for h in range(2):
        loads.append(
            pltpu.make_async_copy(solid_hbm.at[:, :, pl.ds(128 * h, 128)], sp.at[:, h], in_sem.at[6 + h])
        )
    for load in loads:
        load.start()

    barrier = pltpu.get_barrier_semaphore()
    for t in (eight[0], eight[1], eight[2], eight[5], eight[6], eight[7]):
        pl.semaphore_signal(barrier, inc=1, device_id=t, device_id_type=MESH)

    def greet(j, carry):
        pl.semaphore_signal(barrier, inc=1, device_id=(g, lax.rem(d + j, n_dev)), device_id_type=MESH)
        return carry

    lax.fori_loop(1, n_dev, greet, 0)

    for ref, rows in ((kc, (0, 8, 32, 40)), (sc, (0, 8, 32, 40)), (ka, (0, 8, 32, 40)), (kb, (0, 8, 32, 40)), (ea, (0, 8, 32, 40)), (eb, (0, 8, 32, 40))):
        ref[:, :, 0:8, :] = jnp.zeros((GX, 2, 8, 128), F32)
        ref[:, :, 32:40, :] = jnp.zeros((GX, 2, 8, 128), F32)
        ref[0] = jnp.zeros((2, GY, 128), F32)
        ref[GX - 1] = jnp.zeros((2, GY, 128), F32)
    lrecv[d] = lists_ref[...]

    def pack(field, ys, n):
        def one(i, carry):
            for s, r in ((0, 8), (1, 8 + n - 4)):
                for h in range(2):
                    ys[s, i, h, 0:4, :] = field[4 + 2 * i, h, r : r + 4, :]
                    ys[s, i, h, 4:8, :] = field[5 + 2 * i, h, r : r + 4, :]
            return carry

        lax.fori_loop(0, n // 2, one, 0, unroll=4)

    def unpack(field, yr, n, zero):
        def one(i, carry):
            for s, r, edge in ((0, 4, d == 0), (1, 8 + n, d == n_dev - 1)):
                for h in range(2):
                    v = jnp.where(edge, jnp.zeros((8, 128), yr.dtype), yr[s, i, h])
                    field[2 * i, h, r : r + 4, :] = v[0:4]
                    field[2 * i + 1, h, r : r + 4, :] = v[4:8]
            return carry

        lax.fori_loop(0, n // 2 + 4, one, 0, unroll=4)
        if zero:
            @pl.when(g == 0)
            def _():
                field[0:4] = jnp.zeros(field.at[0:4].shape, field.dtype)

            @pl.when(g == n_grp - 1)
            def _():
                field[4 + n : 8 + n] = jnp.zeros(field.at[0:4].shape, field.dtype)

    def halo(e, field, ys, yr, n):
        m = n // 2
        own = pl.ds(8, n)
        low, high = field.at[pl.ds(4, 4), :, own, :], field.at[pl.ds(n, 4), :, own, :]
        to_low, to_high = field.at[pl.ds(0, 4), :, own, :], field.at[pl.ds(4 + n, 4), :, own, :]
        pairs = [
            (ys.at[0, pl.ds(0, 2)], yr.at[1, pl.ds(m + 2, 2)]),
            (low, to_high),
            (ys.at[1, pl.ds(0, 2)], yr.at[0, pl.ds(m + 2, 2)]),
            (ys.at[0], yr.at[1, pl.ds(2, m)]),
            (ys.at[1], yr.at[0, pl.ds(2, m)]),
            (ys.at[0, pl.ds(m - 2, 2)], yr.at[1, pl.ds(0, 2)]),
            (high, to_low),
            (ys.at[1, pl.ds(m - 2, 2)], yr.at[0, pl.ds(0, 2)]),
        ]
        copies = []
        for i in (4, 3, 6, 1, 0, 2, 5, 7):
            src, dst = pairs[i]
            copies.append(
                pltpu.make_async_remote_copy(
                    src_ref=src, dst_ref=dst, send_sem=hs_sem.at[e, i], recv_sem=hr_sem.at[e, i],
                    device_id=eight[i], device_id_type=MESH,
                )
            )
        for c in copies:
            c.start()
        return copies

    def arrive(copies):
        for c in copies:
            c.wait_recv()

    def all_send(src, dst, send_sem, recv_sem):
        def one(j, carry):
            pltpu.make_async_remote_copy(
                src_ref=src, dst_ref=dst.at[d], send_sem=send_sem.at[j], recv_sem=recv_sem.at[d],
                device_id=(g, lax.rem(d + j, n_dev)), device_id_type=MESH,
            ).start()
            return carry

        lax.fori_loop(1, n_dev, one, 0)

    def all_wait(src, dst, send_sem, recv_sem):
        def one(j, carry):
            s = lax.rem(d + n_dev - j, n_dev)
            c = pltpu.make_async_remote_copy(
                src_ref=src, dst_ref=dst.at[s], send_sem=send_sem.at[j], recv_sem=recv_sem.at[s],
                device_id=(g, lax.rem(d + j, n_dev)), device_id_type=MESH,
            )
            c.wait_recv()
            c.wait_send()
            return carry

        lax.fori_loop(1, n_dev, one, 0)

    def z_sum(a, b):
        ra, rb = pltpu.roll(a, 1, 1), pltpu.roll(b, 1, 1)
        sa, sb = pltpu.roll(a, 127, 1), pltpu.roll(b, 127, 1)
        zero = jnp.zeros_like(a)
        za = jnp.where(l0, zero, ra) + jnp.where(l1, sb, sa)
        zb = jnp.where(l0, ra, rb) + jnp.where(l1, zero, sb)
        return za, zb

    def plane(field, x, h, r0, r1):
        return (field[x - 1, h, r0:r1, :] + field[x + 1, h, r0:r1, :]) + (
            field[x, h, r0 - 1 : r1 - 1, :] + field[x, h, r0 + 1 : r1 + 1, :]
        )

    def stencil(field, x, r0, r1, weight):
        a, b = field[x, 0, r0:r1, :], field[x, 1, r0:r1, :]
        za, zb = z_sum(a, b)
        pa, pb = plane(field, x, 0, r0, r1), plane(field, x, 1, r0, r1)
        if weight != 1.0:
            pa, pb = weight * pa, weight * pb
        return (a, b), (pa + za, pb + zb)

    def sweep(src, dst, gain, rhs, x0, x1, r0, r1, weight, unroll):
        def one(x, carry):
            v, s = stencil(src, x, r0, r1, weight)
            for h in range(2):
                dst[x, h, r0:r1, :] = 0.2 * v[h] + rhs[x, h, r0:r1, :] + gain[x, h, r0:r1, :] * s[h]
            return carry

        lax.fori_loop(x0, x1, one, 0, unroll=unroll)

    for k in range(4):
        loads[k].wait()
    pack(c0, ysf.at[0], 32)
    pack(lb, ysl, 32)
    loads[4].wait()
    loads[5].wait()
    pack(ph, ysf.at[1], 32)
    pl.semaphore_wait(barrier, n_dev - 1 + 6)
    all_send(lists_ref, lrecv, ls_sem, lr_sem)
    h_conc = halo(0, c0, ysf.at[0], yrf.at[0], 32)
    h_label = halo(1, lb, ysl, yrl, 32)
    h_phi = halo(2, ph, ysf.at[1], yrf.at[1], 32)

    def own_mid(i, carry):
        for h in range(2):
            total = jnp.zeros((16, 128), F32)
            for x in (0, 1):
                for r in (0, 1):
                    rows = pl.ds(8 + r, 16, stride=2)
                    total = total + lookup(lb[4 + 2 * i + x, h, rows, :], (1.0, 0.3, 0.6)) * c0[4 + 2 * i + x, h, rows, :]
            km[4 + i, h, 8:24, :] = 0.25 * total
        return carry

    lax.fori_loop(0, 16, own_mid, 0, unroll=2)
    pack(km, ysm.at[0], 16)
    h_km = halo(3, km, ysm.at[0], yrm.at[0], 16)

    def own_coarse(dst, src, off):
        def one(i, carry):
            for h in range(2):
                total = jnp.zeros((8, 128), F32)
                for x in (0, 1):
                    for r in (0, 1):
                        total = total + src[off + 2 * i + x, h, pl.ds(8 + r, 8, stride=2), :]
                dst[1 + i, h, 16:24, :] = 0.25 * total
            return carry

        lax.fori_loop(0, 8, one, 0, unroll=2)

    def coarse_exchange(field, k):
        copies = []
        for i, (t, r) in enumerate((((g, dl), 24), ((g, du), 8))):
            copies.append(
                pltpu.make_async_remote_copy(
                    src_ref=field.at[pl.ds(1, 8), :, pl.ds(16, 8), :], dst_ref=field.at[pl.ds(1, 8), :, pl.ds(r, 8), :],
                    send_sem=cs_sem.at[k, i], recv_sem=cr_sem.at[k, i], device_id=t, device_id_type=MESH,
                )
            )
        for c in copies:
            c.start()
        return copies

    def coarse_edges(field):
        @pl.when(d == 0)
        def _():
            field[:, :, 8:16, :] = jnp.zeros((GX, 2, 8, 128), F32)

        @pl.when(d == n_dev - 1)
        def _():
            field[:, :, 24:32, :] = jnp.zeros((GX, 2, 8, 128), F32)

    own_coarse(kc, km, 4)
    x_kc = coarse_exchange(kc, 0)

    arrive(h_conc)
    unpack(c0, yrf.at[0], 32, True)
    arrive(h_label)
    unpack(lb, yrl, 32, False)

    def coeffs(x, carry):
        for h in range(2):
            old = c0[x, h, 4:44, :]
            label = lb[x, h, 4:44, :]
            dif = jnp.where(old > 0.0, lookup(label, (1.5, 0.1, 0.4)), 0.0)
            inv = lookup(label, (1.0 / 10.0, 1.0 / 1.6, 1.0 / 3.4))
            dd[x, h, 4:44, :] = dif * inv
            cc[x, h, 4:44, :] = old * inv
            con = lookup(label, (1.0, 0.3, 0.6)) * old
            kk[x, h, 4:44, :] = con
            rd = 0.8 / (0.05 + 6.0 * con)
            bb[x, h, 4:44, :] = rd
            gg[x, h, 4:44, :] = rd * con
        return carry

    lax.fori_loop(0, FX, coeffs, 0, unroll=2)

    def conc_sweep(src, dst, x0, x1, r0, r1):
        def one(x, carry):
            _, s = stencil(src, x, r0, r1, 1.0)
            for h in range(2):
                dst[x, h, r0:r1, :] = cc[x, h, r0:r1, :] + dd[x, h, r0:r1, :] * s[h]
            return carry

        lax.fori_loop(x0, x1, one, 0, unroll=2)

    conc_sweep(c0, ca, 1, 39, 4, 44)
    conc_sweep(ca, cb, 2, 38, 4, 44)
    conc_sweep(cb, ca, 3, 37, 4, 44)
    conc_sweep(ca, cb, 4, 36, 8, 40)
    outs = []
    for h in range(2):
        outs.append(
            pltpu.make_async_copy(
                cb.at[pl.ds(4, 32), h, pl.ds(8, 32), :], conc_out.at[:, :, pl.ds(128 * h, 128)], out_sem.at[h]
            )
        )
    for o in outs:
        o.start()

    all_wait(lists_ref, lrecv, ls_sem, lr_sem)

    def count(s, carry):
        total = carry
        for r in range(2):
            owner, block = lrecv[s, r : r + 1, :], lrecv[s, r + 2 : r + 3, :]
            place = jnp.where(owner == d, (block & 1) * 32 + ((block >> 1) & 31), -1)
            column = block >> 6
            rows = (lax.broadcasted_iota(jnp.int32, (64, 128), 0) == place).astype(jnp.bfloat16)
            cols = (lax.broadcasted_iota(jnp.int32, (32, 128), 0) == column).astype(jnp.bfloat16)
            total = total + lax.dot_general(
                rows, cols, (((1,), (1,)), ((), ())), preferred_element_type=F32
            )
        return total

    counts = lax.fori_loop(0, n_dev, count, jnp.zeros((64, 32), F32), unroll=4)
    named = jnp.where(counts > 0.0, 1.0, 0.0).astype(jnp.bfloat16)
    spread = (
        lax.broadcasted_iota(jnp.int32, (32, 4096), 1) // 128 == lax.broadcasted_iota(jnp.int32, (32, 4096), 0)
    ).astype(jnp.bfloat16)
    msk[...] = jnp.dot(named, spread, preferred_element_type=F32)

    for k in (6, 7):
        loads[k].wait()
    for x in range(32):
        for h in range(2):
            con = cb[4 + x, h, 8:40, :]
            u = 0.5 * (sp[x, h] - ph[4 + x, h, 8:40, :]) - 0.1 * jnp.log(con)
            kin = lookup(lb[4 + x, h, 8:40, :], (0.2, 1.0, 0.5)) * jnp.sqrt(con)
            val = kin * (jnp.exp(u) - jnp.exp(-u))
            fx[4 + x, h, 8:40, :] = msk[32 * h : 32 * h + 32, 128 * x : 128 * x + 128] * val
    pack(fx, ysf.at[2], 32)
    h_flux = halo(4, fx, ysf.at[2], yrf.at[2], 32)
    for h in range(2):
        outs.append(
            pltpu.make_async_copy(
                fx.at[pl.ds(4, 32), h, pl.ds(8, 32), :], flux_out.at[:, :, pl.ds(128 * h, 128)], out_sem.at[2 + h]
            )
        )
        outs[-1].start()

    arrive(h_phi)
    unpack(ph, yrf.at[1], 32, True)

    def first(x, carry):
        v, s = stencil(ph, x, 4, 44, 1.0)
        for h in range(2):
            rd = bb[x, h, 4:44, :]
            qq[x, h, 4:44, :] = (0.2 + 0.05 * rd) * v[h] + gg[x, h, 4:44, :] * s[h]
        return carry

    lax.fori_loop(1, 39, first, 0, unroll=2)
    arrive(h_km)
    unpack(km, yrm.at[0], 16, True)
    arrive(x_kc)
    coarse_edges(kc)

    def coarse_coeffs(x, carry):
        for h in range(2):
            con = kc[x, h, 8:32, :]
            rd = 0.8 / (0.05 + 2.25 * con)
            rc[x, h, 8:32, :] = rd
            gc[x, h, 8:32, :] = rd * con
            wa[x, h, 8:32, :] = jnp.ones((24, 128), F32)
            ka[x, h, 8:32, :] = con
        return carry

    lax.fori_loop(1, 9, coarse_coeffs, 0)

    def dual(w_in, k_in, w_out, k_out):
        def one(x, carry):
            v, s = stencil(k_in, x, 8, 32, 0.0625)
            for h in range(2):
                w = w_in[x, h, 8:32, :]
                w = w - rc[x, h, 8:32, :] * (0.05 * w + 2.25 * v[h] - s[h])
                w_out[x, h, 8:32, :] = w
                k_out[x, h, 8:32, :] = kc[x, h, 8:32, :] * w
            return carry

        lax.fori_loop(1, 9, one, 0, unroll=4)

    for k in range(4):
        dual(wa, ka, wb, kb)
        dual(wb, kb, wa, ka)

    load = jnp.zeros((8, 128), F32)
    row = lax.broadcasted_iota(jnp.int32, (8, 128), 0)
    lane8 = lax.broadcasted_iota(jnp.int32, (8, 128), 1)
    edge_y = jnp.where(((row == 0) & (d == 0)) | ((row == 7) & (d == n_dev - 1)), 1.0, 0.0)
    for x in range(8):
        for h in range(2):
            edge_z = jnp.where(lane8 == 127 * h, 1.0, 0.0)
            edge_xy = edge_y + (1.0 if x in (0, 7) else 0.0)
            load = load + (0.05 + kc[1 + x, h, 16:24, :] * (0.0625 * edge_xy + edge_z))
    load = jnp.sum(load, axis=0, keepdims=True)

    arrive(h_flux)
    unpack(fx, yrf.at[2], 32, True)

    def second(x, carry):
        for h in range(2):
            rd = bb[x, h, 4:44, :]
            fl = fx[x, h, 4:44, :]
            ca[x, h, 4:44, :] = qq[x, h, 4:44, :] + rd * fl
            src = 0.05 * ph[x, h, 4:44, :] + fl
            qq[x, h, 4:44, :] = src
            bb[x, h, 4:44, :] = rd * src
        return carry

    lax.fori_loop(1, 39, second, 0, unroll=2)
    sweep(ca, p2, gg, bb, 2, 38, 4, 44, 1.0, 2)

    def resid(x, carry):
        v, s = stencil(p2, x, 8, 40, 1.0)
        for h in range(2):
            sp[x - 4, h] = qq[x, h, 8:40, :] - 0.05 * v[h] - kk[x, h, 8:40, :] * (6.0 * v[h] - s[h])
        return carry

    lax.fori_loop(4, 36, resid, 0, unroll=2)

    def down(i, carry):
        for h in range(2):
            total = jnp.zeros((16, 128), F32)
            for x in (0, 1):
                for r in (0, 1):
                    total = total + sp[2 * i + x, h, pl.ds(r, 16, stride=2), :]
            sm[4 + i, h, 8:24, :] = 0.25 * total
        return carry

    lax.fori_loop(0, 16, down, 0, unroll=2)
    pack(sm, ysm.at[1], 16)
    h_sm = halo(5, sm, ysm.at[1], yrm.at[1], 16)

    def mid_coeffs(x, carry):
        for h in range(2):
            con = km[x, h, 4:28, :]
            rd = 0.8 / (0.05 + 3.0 * con)
            bm[x, h, 4:28, :] = rd
            gm[x, h, 4:28, :] = rd * con
        return carry

    lax.fori_loop(0, MX, mid_coeffs, 0, unroll=2)
    arrive(h_sm)
    unpack(sm, yrm.at[1], 16, True)

    def mid_first(x, carry):
        for h in range(2):
            v = bm[x, h, 4:28, :] * sm[x, h, 4:28, :]
            bm[x, h, 4:28, :] = v
            m1[x, h, 4:28, :] = v
        return carry

    lax.fori_loop(0, MX, mid_first, 0, unroll=2)
    sweep(m1, m2, gm, bm, 1, 23, 4, 28, 0.25, 2)

    def mid_resid(x, carry):
        v, s = stencil(m2, x, 8, 24, 0.25)
        for h in range(2):
            m1[x, h, 8:24, :] = sm[x, h, 8:24, :] - 0.05 * v[h] - km[x, h, 8:24, :] * (3.0 * v[h] - s[h])
        return carry

    lax.fori_loop(4, 20, mid_resid, 0, unroll=2)

    own_coarse(sc, m1, 4)
    x_sc = coarse_exchange(sc, 1)
    part = jnp.zeros((8, 128), F32)
    for x in range(8):
        for h in range(2):
            part = part + wa[1 + x, h, 16:24, :] * sc[1 + x, h, 16:24, :]
    part = jnp.sum(part, axis=0, keepdims=True)
    message = jnp.where(row == 0, part, jnp.where(row == 1, load, 0.0))
    psend[...] = message
    precv[d] = message
    all_send(psend, precv, ps_sem, pr_sem)
    arrive(x_sc)
    coarse_edges(sc)

    def coarse_first(x, carry):
        for h in range(2):
            v = rc[x, h, 8:32, :] * sc[x, h, 8:32, :]
            rc[x, h, 8:32, :] = v
            ea[x, h, 8:32, :] = v
        return carry

    lax.fori_loop(1, 9, coarse_first, 0)
    for k in range(3):
        sweep(ea, eb, gc, rc, 1, 9, 8, 32, 0.0625, 4)
        sweep(eb, ea, gc, rc, 1, 9, 8, 32, 0.0625, 4)
    sweep(ea, eb, gc, rc, 1, 9, 8, 32, 0.0625, 4)
    all_wait(psend, precv, ps_sem, pr_sem)

    def gather(s, carry):
        return carry + precv[s]

    sums = lax.fori_loop(0, n_dev, gather, jnp.zeros((8, 128), F32), unroll=4)
    sums = jnp.sum(sums, axis=1, keepdims=True)
    shift = jnp.broadcast_to(sums[0:1] / sums[1:2], (8, 128))
    for x in range(8):
        for h in range(2):
            ec[4 + x, h, 8:16, :] = eb[1 + x, h, 16:24, :] + shift
    pack(ec, yse, 8)
    h_ec = halo(6, ec, yse, yre, 8)
    arrive(h_ec)
    unpack(ec, yre, 8, True)

    def mid_up(i, carry):
        for h in range(2):
            v = ec[i, h, 6:18, :]
            for x in (0, 1):
                for r in (0, 1):
                    rows = pl.ds(4 + r, 12, stride=2)
                    m2[2 * i - 4 + x, h, rows, :] = m2[2 * i - 4 + x, h, rows, :] + v
        return carry

    lax.fori_loop(2, 14, mid_up, 0, unroll=2)
    sweep(m2, m1, gm, bm, 2, 22, 4, 28, 0.25, 2)
    sweep(m1, m2, gm, bm, 3, 21, 4, 28, 0.25, 2)

    def fine_up(i, carry):
        for h in range(2):
            v = m2[i, h, 6:26, :]
            for x in (0, 1):
                for r in (0, 1):
                    rows = pl.ds(4 + r, 20, stride=2)
                    p2[2 * i - 4 + x, h, rows, :] = p2[2 * i - 4 + x, h, rows, :] + v
        return carry

    lax.fori_loop(3, 21, fine_up, 0, unroll=2)
    sweep(p2, ca, gg, bb, 3, 37, 4, 44, 1.0, 2)
    sweep(ca, p2, gg, bb, 4, 36, 8, 40, 1.0, 2)
    for h in range(2):
        outs.append(
            pltpu.make_async_copy(
                p2.at[pl.ds(4, 32), h, pl.ds(8, 32), :], pot_out.at[:, :, pl.ds(128 * h, 128)], out_sem.at[4 + h]
            )
        )
        outs[-1].start()
    for copies in (h_conc, h_label, h_phi, h_km, h_flux, h_sm, h_ec, x_kc, x_sc):
        for c in copies:
            c.wait_send()
    for o in outs:
        o.wait()


def body(conc_old, phi_old, solid_pot, phase_label, iface_block, iface_owner):
    n_grp, n_dev = lax.axis_size("grp"), lax.axis_size("dev")
    lists = jnp.concatenate(
        [iface_owner.reshape(2, 128), iface_block.reshape(2, 128), jnp.zeros((4, 128), jnp.int32)], axis=0
    )
    fine = pltpu.VMEM((FX, 2, FY, 128), F32)
    mid = pltpu.VMEM((MX, 2, MY, 128), F32)
    coarse = pltpu.VMEM((GX, 2, GY, 128), F32)
    dma = pltpu.SemaphoreType.DMA
    out = jax.ShapeDtypeStruct(conc_old.shape, F32)
    hbm = pl.BlockSpec(memory_space=pl.ANY)
    return pl.pallas_call(
        functools.partial(kernel, n_grp, n_dev),
        out_shape=(out, out, out),
        in_specs=[hbm, hbm, hbm, hbm, pl.BlockSpec(memory_space=pltpu.VMEM)],
        out_specs=(hbm, hbm, hbm),
        scratch_shapes=[
            fine, pltpu.VMEM((FX, 2, FY, 128), jnp.int32), fine, pltpu.VMEM((32, 2, 32, 128), F32),
            fine, fine, fine, fine, fine, fine, fine, fine, fine, fine,
            mid, mid, mid, mid, mid, mid,
            coarse, coarse, coarse, coarse, coarse, coarse, coarse, coarse, coarse, coarse,
            pltpu.VMEM((EX, 2, EY, 128), F32),
            pltpu.VMEM((3, 2, 16, 2, 8, 128), F32), pltpu.VMEM((3, 2, 20, 2, 8, 128), F32),
            pltpu.VMEM((2, 16, 2, 8, 128), jnp.int32), pltpu.VMEM((2, 20, 2, 8, 128), jnp.int32),
            pltpu.VMEM((2, 2, 8, 2, 8, 128), F32), pltpu.VMEM((2, 2, 12, 2, 8, 128), F32),
            pltpu.VMEM((2, 4, 2, 8, 128), F32), pltpu.VMEM((2, 8, 2, 8, 128), F32),
            pltpu.VMEM((n_dev, 8, 128), jnp.int32), pltpu.VMEM((64, 4096), F32),
            pltpu.VMEM((8, 128), F32), pltpu.VMEM((n_dev, 8, 128), F32),
            dma((8,)), dma((6,)), dma((7, 8)), dma((7, 8)), dma((2, 2)), dma((2, 2)),
            dma((n_dev,)), dma((n_dev,)), dma((n_dev,)), dma((n_dev,)),
        ],
        compiler_params=pltpu.CompilerParams(
            collective_id=0, has_side_effects=True, vmem_limit_bytes=56 * 1024 * 1024
        ),
    )(conc_old, phi_old, solid_pot, phase_label, lists)


def solution(mesh):
    split = P("grp", "dev", None)
    return jax.shard_map(
        body,
        mesh=mesh,
        in_specs=(split, split, split, split, P("grp", "dev"), split),
        out_specs=(split, split, split),
        check_vma=False,
    )
```

time: 496 us -> 86.6 us (0.17)
  the two profiles are of different devices: /device:TPU:14 before, /device:TPU:1 now
where the time goes in v1:
time: 86.6 us; the launch traced here: 86.4 us
  Pallas kernels  79.4 us (92%)
  local copies, waits for them, and re-layouts  5.65 us (7%)
    pallas_call x1, Pallas kernels, body(): pl.pallas_call(functools.partial(kernel, n_grp, n_dev), out_shape=(out, o...  79.4 us
    unnamed x11, local copies, waits for them, and re-layouts  5.57 us

profile of v1, /device:TPU:1, one launch (start us, length us, event | category | flops | bytes accessed | tf_op | source)
XLA Modules:
  0.0 86.4 jit_solution(7810086423143474417)
XLA Ops:
  0.6 0.0 copy-start.3
  0.7 0.0 copy-start.2
  0.7 0.1 pad.2.clone
  0.7 0.6 copy-done.3
  1.3 0.0 copy-done.2
  1.3 0.7 add_add_fusion.lists_ref
  2.0 79.4 %shard_map.85 = (f32[32,32,256]{2,1,0:T(8,128)}, f32[32,32,256]{2,1,0:T(8,128)}, f32[32,32,256]{2,1,0:T(8,128)}) custom-call(f32[32,32,256]{2,1,0:T(8,128)} %conc_hbm.1, f32[32,32,256]{2,1,0:T(8,128)} %phi_hbm.1, f32[32,32,256]{2,1,0:T(8,128)} %solid_hbm.1, s32[32,32,256]{2,1,0:T(8,128)} %label_hbm.1, s32[8,128]{1,0:T(8,128)} %add_add_fusion.lists_ref), custom_call_target="tpu_custom_call" | custom-call | tf_op jit(solution)/shard_map/pallas_call | solution.py:560
  81.4 0.0 copy-start.1
  81.5 2.4 %copy.12 = f32[32,32,256]{2,1,0:T(8,128)} copy(f32[32,32,256]{2,1,0:T(8,128)} %get-tuple-element.6) | data formatting | bytes 2097152
  83.9 0.0 copy-done.1
  83.9 0.0 copy-start
  83.9 1.0 %copy.13 = f32[32,32,256]{2,1,0:T(8,128)} copy(f32[32,32,256]{2,1,0:T(8,128)S(1)} %copy-done.1) | data formatting | bytes 2097152
  84.8 0.6 copy-done
  85.5 1.0 %copy.14 = f32[32,32,256]{2,1,0:T(8,128)} copy(f32[32,32,256]{2,1,0:T(8,128)S(1)} %copy-done) | data formatting | bytes 2097152
  (1 shorter events, 0.0 us)
Async XLA Ops:
  0.6 0.7 copy-start.3
  0.7 0.7 copy-start.2
  81.4 2.4 %copy-start.1 = (f32[32,32,256]{2,1,0:T(8,128)S(1)}, f32[32,32,256]{2,1,0:T(8,128)}, u32[]{:S(2)}) copy-start(f32[32,32,256]{2,1,0:T(8,128)} %get-tuple-element.7) | copy-start | bytes 3145732
  83.9 1.6 %copy-start = (f32[32,32,256]{2,1,0:T(8,128)S(1)}, f32[32,32,256]{2,1,0:T(8,128)}, u32[]{:S(2)}) copy-start(f32[32,32,256]{2,1,0:T(8,128)} %get-tuple-element.8) | copy-start | bytes 3145732

commit v2 on v1

v2 whole, which is shorter than its diff:
```python
import functools

import jax
import jax.numpy as jnp
from jax import lax
from jax.experimental import pallas as pl
from jax.experimental.pallas import tpu as pltpu
from jax.sharding import PartitionSpec as P

MESH = pl.DeviceIdType.MESH
F32 = jnp.float32

FX, FY = 40, 48
MX, MY = 24, 32
EX, EY = 16, 24
GX, GY = 10, 40


def lookup(label, table):
    return jnp.where(label == 0, table[0], jnp.where(label == 1, table[1], table[2])).astype(F32)


def kernel(
    n_grp,
    n_dev,
    conc_hbm,
    phi_hbm,
    solid_hbm,
    label_hbm,
    owner_hbm,
    block_hbm,
    conc_out,
    flux_out,
    pot_out,
    c0, lb, ph, sp, ca, cb, rs, dd, cc, kk, gg, qq, bb, fx, p2,
    sm, km, gm, bm, m1, m2, mu,
    kc, rc, gc, wa, wb, ka, kb, sc, ea, eb,
    ec,
    ysc, yrc, ysl, yrl, ysp, yrp, ysf, yrf, ysu, yru, ysk, yrk, yss, yrs, ysm, yrm, yse, yre,
    lists, lrecv, msk, psend, precv, shifts,
    in_sem, hs_sem, hr_sem, cs_sem, cr_sem, ls_sem, lr_sem, ps_sem, pr_sem, ss_sem, sr_sem,
):
    g = lax.axis_index("grp")
    d = lax.axis_index("dev")
    gu, gd = lax.rem(g + 1, n_grp), lax.rem(g + n_grp - 1, n_grp)
    du, dl = lax.rem(d + 1, n_dev), lax.rem(d + n_dev - 1, n_dev)
    eight = [(gd, dl), (gd, d), (gd, du), (g, dl), (g, du), (gu, dl), (gu, d), (gu, du)]
    lane = lax.broadcasted_iota(jnp.int32, (1, 128), 1)
    l0, l1 = lane == 0, lane == 127

    loads = []
    for k, (src, dst) in enumerate(((conc_hbm, c0), (label_hbm, lb), (phi_hbm, ph))):
        for h in range(2):
            loads.append(
                pltpu.make_async_copy(
                    src.at[:, :, pl.ds(128 * h, 128)], dst.at[pl.ds(4, 32), h, pl.ds(8, 32), :], in_sem.at[2 * k + h]
                )
            )
    for h in range(2):
        loads.append(
            pltpu.make_async_copy(solid_hbm.at[:, :, pl.ds(128 * h, 128)], sp.at[:, h], in_sem.at[6 + h])
        )
    for k, src in enumerate((owner_hbm, block_hbm)):
        loads.append(pltpu.make_async_copy(src, lists.at[k], in_sem.at[8 + k]))
    for load in loads:
        load.start()

    barrier = pltpu.get_barrier_semaphore()
    for t in (eight[0], eight[1], eight[2], eight[5], eight[6], eight[7]):
        pl.semaphore_signal(barrier, inc=1, device_id=t, device_id_type=MESH)

    def greet(j, carry):
        pl.semaphore_signal(barrier, inc=1, device_id=(g, lax.rem(d + j, n_dev)), device_id_type=MESH)
        return carry

    lax.fori_loop(1, n_dev, greet, 0)

    for ref, rows in ((kc, (0, 8, 32, 40)), (sc, (0, 8, 32, 40)), (ka, (0, 8, 32, 40)), (kb, (0, 8, 32, 40)), (ea, (0, 8, 32, 40)), (eb, (0, 8, 32, 40))):
        ref[:, :, 0:8, :] = jnp.zeros((GX, 2, 8, 128), F32)
        ref[:, :, 32:40, :] = jnp.zeros((GX, 2, 8, 128), F32)
        ref[0] = jnp.zeros((2, GY, 128), F32)
        ref[GX - 1] = jnp.zeros((2, GY, 128), F32)

    def pack(field, ys, n, deep):
        def one(x, carry):
            for s, r in ((0, 8), (1, 8 + n - deep)):
                for h in range(2):
                    ys[s, h, pl.ds(deep * x, deep), :] = field[4 + x, h, r : r + deep, :]
            return carry

        lax.fori_loop(0, n, one, 0, unroll=8)

    def unpack(field, yr, n, deep, wide, zero):
        edge_rows = 8 * ((4 * deep + 7) // 8)

        def one(x, carry):
            for s, r, edge in ((0, 8 - deep, d == 0), (1, 8 + n, d == n_dev - 1)):
                for h in range(2):
                    v = yr[s, h, pl.ds(edge_rows + deep * (x - 4), deep), :]
                    field[x, h, r : r + deep, :] = jnp.where(edge, jnp.zeros_like(v), v)
            return carry

        lax.fori_loop(4 - wide, 4 + n + wide, one, 0, unroll=8)
        if zero:
            @pl.when(g == 0)
            def _():
                field[4 - wide : 4] = jnp.zeros(field.at[4 - wide : 4].shape, field.dtype)

            @pl.when(g == n_grp - 1)
            def _():
                field[4 + n : 4 + n + wide] = jnp.zeros(field.at[4 - wide : 4].shape, field.dtype)

    def halo(e, field, ys, yr, n, deep, wide):
        c = 8 * ((4 * deep + 7) // 8)
        m = n * deep
        own = pl.ds(8, n)
        low, high = field.at[pl.ds(4, wide), :, own, :], field.at[pl.ds(4 + n - wide, wide), :, own, :]
        to_low, to_high = field.at[pl.ds(4 - wide, wide), :, own, :], field.at[pl.ds(4 + n, wide), :, own, :]
        first, last, after, before = pl.ds(0, c), pl.ds(m - c, c), pl.ds(c + m, c), pl.ds(0, c)
        pairs = [
            (ys.at[0, :, first], yr.at[1, :, after]),
            (low, to_high),
            (ys.at[1, :, first], yr.at[0, :, after]),
            (ys.at[0], yr.at[1, :, pl.ds(c, m)]),
            (ys.at[1], yr.at[0, :, pl.ds(c, m)]),
            (ys.at[0, :, last], yr.at[1, :, before]),
            (high, to_low),
            (ys.at[1, :, last], yr.at[0, :, before]),
        ]
        copies = []
        for i in (0, 2, 5, 7, 4, 3, 6, 1):
            src, dst = pairs[i]
            copies.append(
                pltpu.make_async_remote_copy(
                    src_ref=src, dst_ref=dst, send_sem=hs_sem.at[e, i], recv_sem=hr_sem.at[e, i],
                    device_id=eight[i], device_id_type=MESH,
                )
            )
        for c in copies:
            c.start()
        return copies

    def sent(copies):
        for c in copies:
            c.wait_send()

    def arrive(copies):
        for c in copies:
            c.wait_recv()

    def all_send(src, dst, send_sem, recv_sem):
        def one(j, carry):
            pltpu.make_async_remote_copy(
                src_ref=src, dst_ref=dst.at[d], send_sem=send_sem.at[j], recv_sem=recv_sem.at[d],
                device_id=(g, lax.rem(d + j, n_dev)), device_id_type=MESH,
            ).start()
            return carry

        lax.fori_loop(1, n_dev, one, 0)

    def all_wait(src, dst, send_sem, recv_sem):
        def one(j, carry):
            s = lax.rem(d + n_dev - j, n_dev)
            c = pltpu.make_async_remote_copy(
                src_ref=src, dst_ref=dst.at[s], send_sem=send_sem.at[j], recv_sem=recv_sem.at[s],
                device_id=(g, lax.rem(d + j, n_dev)), device_id_type=MESH,
            )
            c.wait_recv()
            c.wait_send()
            return carry

        lax.fori_loop(1, n_dev, one, 0)

    def z_sum(a, b):
        ra, rb = pltpu.roll(a, 1, 1), pltpu.roll(b, 1, 1)
        sa, sb = pltpu.roll(a, 127, 1), pltpu.roll(b, 127, 1)
        zero = jnp.zeros_like(a)
        za = jnp.where(l0, zero, ra) + jnp.where(l1, sb, sa)
        zb = jnp.where(l0, ra, rb) + jnp.where(l1, zero, sb)
        return za, zb

    def plane(field, x, h, r0, r1):
        return (field[x - 1, h, r0:r1, :] + field[x + 1, h, r0:r1, :]) + (
            field[x, h, r0 - 1 : r1 - 1, :] + field[x, h, r0 + 1 : r1 + 1, :]
        )

    def stencil(field, x, r0, r1, weight):
        a, b = field[x, 0, r0:r1, :], field[x, 1, r0:r1, :]
        za, zb = z_sum(a, b)
        pa, pb = plane(field, x, 0, r0, r1), plane(field, x, 1, r0, r1)
        if weight != 1.0:
            pa, pb = weight * pa, weight * pb
        return (a, b), (pa + za, pb + zb)

    def sweep(src, dst, gain, rhs, x0, x1, r0, r1, weight, unroll):
        def one(x, carry):
            v, s = stencil(src, x, r0, r1, weight)
            for h in range(2):
                dst[x, h, r0:r1, :] = 0.2 * v[h] + rhs[x, h, r0:r1, :] + gain[x, h, r0:r1, :] * s[h]
            return carry

        lax.fori_loop(x0, x1, one, 0, unroll=unroll)

    for k in range(4):
        loads[k].wait()
    pack(c0, ysc, 32, 4)
    pack(lb, ysl, 32, 3)

    def conc_coeffs(x, r0, r1):
        for h in range(2):
            old = c0[x, h, r0:r1, :]
            label = lb[x, h, r0:r1, :]
            dd[x, h, r0:r1, :] = jnp.where(old > 0.0, lookup(label, (1.5 / 10.0, 0.1 / 1.6, 0.4 / 3.4)), 0.0)
            cc[x, h, r0:r1, :] = old * lookup(label, (1.0 / 10.0, 1.0 / 1.6, 1.0 / 3.4))

    def pot_coeffs(x, r0, r1):
        for h in range(2):
            con = lookup(lb[x, h, r0:r1, :], (1.0, 0.3, 0.6)) * c0[x, h, r0:r1, :]
            rd = 0.8 / (0.05 + 6.0 * con)
            kk[x, h, r0:r1, :] = con
            bb[x, h, r0:r1, :] = rd
            gg[x, h, r0:r1, :] = rd * con

    def each(lo, hi, unroll, *fns):
        def one(x, carry):
            for fn in fns:
                fn(x)
            return carry

        lax.fori_loop(lo, hi, one, 0, unroll=unroll)

    each(4, 36, 4, lambda x: conc_coeffs(x, 8, 40), lambda x: pot_coeffs(x, 8, 40))
    loads[4].wait()
    loads[5].wait()
    pack(ph, ysp, 32, 3)
    loads[8].wait()
    loads[9].wait()
    lrecv[d] = lists[...]

    def own_mid(i, carry):
        for h in range(2):
            total = jnp.zeros((16, 128), F32)
            for x in (0, 1):
                for r in (0, 1):
                    rows = pl.ds(8 + r, 16, stride=2)
                    total = total + kk[4 + 2 * i + x, h, rows, :]
            km[4 + i, h, 8:24, :] = 0.25 * total
        return carry

    lax.fori_loop(0, 16, own_mid, 0, unroll=4)
    pack(km, ysk, 16, 2)

    def own_coarse(dst, src, off):
        def one(i, carry):
            for h in range(2):
                total = jnp.zeros((8, 128), F32)
                for x in (0, 1):
                    for r in (0, 1):
                        total = total + src[off + 2 * i + x, h, pl.ds(8 + r, 8, stride=2), :]
                dst[1 + i, h, 16:24, :] = 0.25 * total
            return carry

        lax.fori_loop(0, 8, one, 0, unroll=8)

    def coarse_exchange(field, k):
        copies = []
        for i, (t, r) in enumerate((((g, dl), 24), ((g, du), 8))):
            copies.append(
                pltpu.make_async_remote_copy(
                    src_ref=field.at[pl.ds(1, 8), :, pl.ds(16, 8), :], dst_ref=field.at[pl.ds(1, 8), :, pl.ds(r, 8), :],
                    send_sem=cs_sem.at[k, i], recv_sem=cr_sem.at[k, i], device_id=t, device_id_type=MESH,
                )
            )
        for c in copies:
            c.start()
        return copies

    def coarse_edges(field):
        @pl.when(d == 0)
        def _():
            field[:, :, 8:16, :] = jnp.zeros((GX, 2, 8, 128), F32)

        @pl.when(d == n_dev - 1)
        def _():
            field[:, :, 24:32, :] = jnp.zeros((GX, 2, 8, 128), F32)

    own_coarse(kc, km, 4)

    pl.semaphore_wait(barrier, n_dev - 1 + 6)
    h_conc = halo(0, c0, ysc, yrc, 32, 4, 4)
    h_label = halo(1, lb, ysl, yrl, 32, 3, 3)
    all_send(lists, lrecv, ls_sem, lr_sem)
    for k in (6, 7):
        loads[k].wait()
    all_wait(lists, lrecv, ls_sem, lr_sem)

    def count(s, carry):
        total = carry
        for r in range(2):
            owner, block = lrecv[s, 0, r : r + 1, :], lrecv[s, 1, r : r + 1, :]
            place = jnp.where(owner == d, (block & 1) * 32 + ((block >> 1) & 31), -1)
            column = block >> 6
            rows = (lax.broadcasted_iota(jnp.int32, (64, 128), 0) == place).astype(jnp.bfloat16)
            cols = (lax.broadcasted_iota(jnp.int32, (32, 128), 0) == column).astype(jnp.bfloat16)
            total = total + lax.dot_general(
                rows, cols, (((1,), (1,)), ((), ())), preferred_element_type=F32
            )
        return total

    counts = lax.fori_loop(0, n_dev, count, jnp.zeros((64, 32), F32), unroll=8)
    named = jnp.where(counts > 0.0, 1.0, 0.0).astype(jnp.bfloat16)
    spread = (
        lax.broadcasted_iota(jnp.int32, (32, 4096), 1) // 128 == lax.broadcasted_iota(jnp.int32, (32, 4096), 0)
    ).astype(jnp.bfloat16)
    msk[...] = jnp.dot(named, spread, preferred_element_type=F32)
    arrive(h_conc)
    unpack(c0, yrc, 32, 4, 4, True)
    arrive(h_label)
    unpack(lb, yrl, 32, 3, 3, False)
    h_phi = halo(2, ph, ysp, yrp, 32, 3, 3)
    x_kc = coarse_exchange(kc, 0)
    each(1, 4, 3, lambda x: conc_coeffs(x, 0, 48))
    each(36, 39, 3, lambda x: conc_coeffs(x, 0, 48))
    each(4, 36, 8, lambda x: conc_coeffs(x, 0, 8), lambda x: conc_coeffs(x, 40, 48))

    def conc_sweep(src, dst, x0, x1, r0, r1, unroll):
        def one(x, carry):
            _, s = stencil(src, x, r0, r1, 1.0)
            for h in range(2):
                v = cc[x, h, r0:r1, :] + dd[x, h, r0:r1, :] * s[h]
                if dst is None:
                    conc_out[x - 4, :, 128 * h : 128 * h + 128] = v
                else:
                    dst[x, h, r0:r1, :] = v
            return carry

        lax.fori_loop(x0, x1, one, 0, unroll=unroll)

    conc_sweep(c0, ca, 1, 39, 4, 44, 19)
    conc_sweep(ca, cb, 2, 38, 4, 44, 18)
    conc_sweep(cb, ca, 3, 37, 4, 44, 17)
    conc_sweep(ca, None, 4, 36, 8, 40, 16)

    for x in range(32):
        for h in range(2):
            con = conc_out[x, :, 128 * h : 128 * h + 128]
            u = 0.5 * (sp[x, h] - ph[4 + x, h, 8:40, :]) - 0.1 * jnp.log(con)
            kin = lookup(lb[4 + x, h, 8:40, :], (0.2, 1.0, 0.5)) * jnp.sqrt(con)
            val = kin * (jnp.exp(u) - jnp.exp(-u))
            val = msk[32 * h : 32 * h + 32, 128 * x : 128 * x + 128] * val
            fx[4 + x, h, 8:40, :] = val
            flux_out[x, :, 128 * h : 128 * h + 128] = val
    pack(fx, ysf, 32, 2)
    h_flux = halo(4, fx, ysf, yrf, 32, 2, 2)

    each(2, 4, 2, lambda x: pot_coeffs(x, 0, 48))
    each(36, 38, 2, lambda x: pot_coeffs(x, 0, 48))
    each(4, 36, 8, lambda x: pot_coeffs(x, 0, 8), lambda x: pot_coeffs(x, 40, 48))
    arrive(h_phi)
    unpack(ph, yrp, 32, 3, 3, True)

    def first(x, carry):
        v, s = stencil(ph, x, 4, 44, 1.0)
        for h in range(2):
            rd = bb[x, h, 4:44, :]
            qq[x, h, 4:44, :] = (0.2 + 0.05 * rd) * v[h] + gg[x, h, 4:44, :] * s[h]
        return carry

    lax.fori_loop(2, 38, first, 0, unroll=12)
    arrive(x_kc)
    coarse_edges(kc)

    def coarse_coeffs(x, carry):
        for h in range(2):
            con = kc[x, h, 8:32, :]
            rd = 0.8 / (0.05 + 2.25 * con)
            rc[x, h, 8:32, :] = rd
            gc[x, h, 8:32, :] = rd * con
            wa[x, h, 8:32, :] = jnp.ones((24, 128), F32)
            ka[x, h, 8:32, :] = con
        return carry

    lax.fori_loop(1, 9, coarse_coeffs, 0, unroll=4)

    def dual(w_in, k_in, w_out, k_out):
        def one(x, carry):
            v, s = stencil(k_in, x, 8, 32, 0.0625)
            for h in range(2):
                w = w_in[x, h, 8:32, :]
                w = w - rc[x, h, 8:32, :] * (0.05 * w + 2.25 * v[h] - s[h])
                w_out[x, h, 8:32, :] = w
                k_out[x, h, 8:32, :] = kc[x, h, 8:32, :] * w
            return carry

        lax.fori_loop(1, 9, one, 0, unroll=8)

    for k in range(4):
        dual(wa, ka, wb, kb)
        dual(wb, kb, wa, ka)

    load = jnp.zeros((8, 128), F32)
    row = lax.broadcasted_iota(jnp.int32, (8, 128), 0)
    lane8 = lax.broadcasted_iota(jnp.int32, (8, 128), 1)
    edge_y = jnp.where(((row == 0) & (d == 0)) | ((row == 7) & (d == n_dev - 1)), 1.0, 0.0)
    for x in range(8):
        for h in range(2):
            edge_z = jnp.where(lane8 == 127 * h, 1.0, 0.0)
            edge_xy = edge_y + (1.0 if x in (0, 7) else 0.0)
            load = load + (0.05 + kc[1 + x, h, 16:24, :] * (0.0625 * edge_xy + edge_z))
    load = jnp.sum(load, axis=0, keepdims=True)
    row2 = lax.broadcasted_iota(jnp.int32, (2, 128), 0)

    arrive(h_flux)
    unpack(fx, yrf, 32, 2, 2, True)
    h_km = halo(3, km, ysk, yrk, 16, 2, 2)

    def second(x, carry):
        for h in range(2):
            rd = bb[x, h, 4:44, :]
            fl = fx[x, h, 4:44, :]
            ca[x, h, 4:44, :] = qq[x, h, 4:44, :] + rd * fl
            src = 0.05 * ph[x, h, 4:44, :] + fl
            qq[x, h, 4:44, :] = src
            bb[x, h, 4:44, :] = rd * src
        return carry

    lax.fori_loop(2, 38, second, 0, unroll=6)
    sweep(ca, p2, gg, bb, 3, 37, 4, 44, 1.0, 17)

    def resid(x, carry):
        v, s = stencil(p2, x, 8, 40, 1.0)
        for h in range(2):
            rs[x - 4, h] = qq[x, h, 8:40, :] - 0.05 * v[h] - kk[x, h, 8:40, :] * (6.0 * v[h] - s[h])
        return carry

    lax.fori_loop(4, 36, resid, 0, unroll=16)

    def down(i, carry):
        for h in range(2):
            total = jnp.zeros((16, 128), F32)
            for x in (0, 1):
                for r in (0, 1):
                    total = total + rs[2 * i + x, h, pl.ds(r, 16, stride=2), :]
            sm[4 + i, h, 8:24, :] = 0.25 * total
        return carry

    lax.fori_loop(0, 16, down, 0, unroll=8)
    pack(sm, yss, 16, 2)
    h_sm = halo(5, sm, yss, yrs, 16, 2, 2)
    pack(p2, ysu, 32, 2)
    arrive(h_km)
    unpack(km, yrk, 16, 2, 2, True)

    def mid_coeffs(x, carry):
        for h in range(2):
            con = km[x, h, 4:28, :]
            rd = 0.8 / (0.05 + 3.0 * con)
            bm[x, h, 4:28, :] = rd
            gm[x, h, 4:28, :] = rd * con
        return carry

    lax.fori_loop(2, 22, mid_coeffs, 0, unroll=5)
    arrive(h_sm)
    unpack(sm, yrs, 16, 2, 2, True)
    h_p2 = halo(7, p2, ysu, yru, 32, 2, 2)

    def mid_first(x, carry):
        for h in range(2):
            v = bm[x, h, 4:28, :] * sm[x, h, 4:28, :]
            bm[x, h, 4:28, :] = v
            m1[x, h, 4:28, :] = v
        return carry

    lax.fori_loop(2, 22, mid_first, 0, unroll=10)
    sweep(m1, m2, gm, bm, 3, 21, 4, 28, 0.25, 18)

    def mid_resid(x, carry):
        v, s = stencil(m2, x, 8, 24, 0.25)
        for h in range(2):
            m1[x, h, 8:24, :] = sm[x, h, 8:24, :] - 0.05 * v[h] - km[x, h, 8:24, :] * (3.0 * v[h] - s[h])
            mu[x, h, 8:24, :] = v[h]
        return carry

    lax.fori_loop(4, 20, mid_resid, 0, unroll=16)

    own_coarse(sc, m1, 4)
    x_sc = coarse_exchange(sc, 1)
    part = jnp.zeros((8, 128), F32)
    for x in range(8):
        for h in range(2):
            part = part + wa[1 + x, h, 16:24, :] * sc[1 + x, h, 16:24, :]
    part = jnp.sum(part, axis=0, keepdims=True)
    message = jnp.where(row2 == 0, jnp.broadcast_to(part, (2, 128)), jnp.broadcast_to(load, (2, 128)))
    psend[...] = message
    precv[d] = message
    all_send(psend, precv, ps_sem, pr_sem)
    pack(mu, ysm, 16, 3)
    h_mu = halo(8, mu, ysm, yrm, 16, 3, 3)
    arrive(x_sc)
    coarse_edges(sc)

    def coarse_first(x, carry):
        for h in range(2):
            v = rc[x, h, 8:32, :] * sc[x, h, 8:32, :]
            rc[x, h, 8:32, :] = v
            ea[x, h, 8:32, :] = v
        return carry

    lax.fori_loop(1, 9, coarse_first, 0, unroll=8)
    for k in range(3):
        sweep(ea, eb, gc, rc, 1, 9, 8, 32, 0.0625, 8)
        sweep(eb, ea, gc, rc, 1, 9, 8, 32, 0.0625, 8)
    sweep(ea, eb, gc, rc, 1, 9, 8, 32, 0.0625, 8)
    for x in range(8):
        for h in range(2):
            ec[4 + x, h, 8:16, :] = eb[1 + x, h, 16:24, :]
    pack(ec, yse, 8, 2)
    h_ec = halo(6, ec, yse, yre, 8, 2, 2)
    all_wait(psend, precv, ps_sem, pr_sem)

    def gather(s, carry):
        return carry + precv[s]

    sums = lax.fori_loop(0, n_dev, gather, jnp.zeros((2, 128), F32), unroll=8)
    sums = jnp.sum(sums, axis=1, keepdims=True)
    shifts[1] = jnp.broadcast_to(sums[0:1] / sums[1:2], (8, 128))
    x_shift = []
    for k, (t, i) in enumerate((((gd, d), 2), ((gu, d), 0))):
        x_shift.append(
            pltpu.make_async_remote_copy(
                src_ref=shifts.at[1], dst_ref=shifts.at[i], send_sem=ss_sem.at[k], recv_sem=sr_sem.at[k],
                device_id=t, device_id_type=MESH,
            )
        )
    for c in x_shift:
        c.start()
    arrive(h_mu)
    sent(h_mu)
    unpack(mu, yrm, 16, 3, 3, True)
    arrive(h_p2)
    sent(h_p2)
    unpack(p2, yru, 32, 2, 2, True)
    arrive(h_ec)
    unpack(ec, yre, 8, 2, 2, True)
    arrive(x_shift)

    row12 = lax.broadcasted_iota(jnp.int32, (12, 128), 0)
    inside = jnp.where(((row12 < 2) & (d == 0)) | ((row12 >= 10) & (d == n_dev - 1)), 0.0, 1.0)
    own_shift = inside * shifts[1, 0:1, :]
    low_shift = jnp.where(g == 0, jnp.zeros((12, 128), F32), inside * shifts[0, 0:1, :])
    high_shift = jnp.where(g == n_grp - 1, jnp.zeros((12, 128), F32), inside * shifts[2, 0:1, :])
    for i in range(2, 14):
        for h in range(2):
            v = ec[i, h, 6:18, :] + (low_shift if i < 4 else own_shift if i < 12 else high_shift)
            for x in (0, 1):
                if not 1 <= 2 * i - 4 + x < 23:
                    continue
                for r in (0, 1):
                    rows = pl.ds(4 + r, 12, stride=2)
                    mu[2 * i - 4 + x, h, rows, :] = mu[2 * i - 4 + x, h, rows, :] + v
    sweep(mu, m1, gm, bm, 2, 22, 4, 28, 0.25, 10)
    sweep(m1, m2, gm, bm, 3, 21, 4, 28, 0.25, 18)

    def fine_up(i, carry):
        for h in range(2):
            v = m2[i, h, 6:26, :]
            for x in (0, 1):
                for r in (0, 1):
                    rows = pl.ds(4 + r, 20, stride=2)
                    p2[2 * i - 4 + x, h, rows, :] = p2[2 * i - 4 + x, h, rows, :] + v
        return carry

    lax.fori_loop(3, 21, fine_up, 0, unroll=6)
    sweep(p2, ca, gg, bb, 3, 37, 4, 44, 1.0, 17)

    def last(x, carry):
        v, s = stencil(ca, x, 8, 40, 1.0)
        for h in range(2):
            new = 0.2 * v[h] + bb[x, h, 8:40, :] + gg[x, h, 8:40, :] * s[h]
            pot_out[x - 4, :, 128 * h : 128 * h + 128] = new
        return carry

    lax.fori_loop(4, 36, last, 0, unroll=16)
    for copies in (h_conc, h_label, h_phi, h_km, h_flux, h_sm, h_ec, x_kc, x_sc, x_shift):
        sent(copies)


def store(conc, flux, pot, conc_out, flux_out, pot_out, sem):
    copies = [
        pltpu.make_async_copy(src, dst, sem.at[k])
        for k, (src, dst) in enumerate(((conc, conc_out), (flux, flux_out), (pot, pot_out)))
    ]
    for c in copies:
        c.start()
    for c in copies:
        c.wait()


def body(conc_old, phi_old, solid_pot, phase_label, iface_block, iface_owner):
    n_grp, n_dev = lax.axis_size("grp"), lax.axis_size("dev")
    fine = pltpu.VMEM((FX, 2, FY, 128), F32)
    mid = pltpu.VMEM((MX, 2, MY, 128), F32)
    coarse = pltpu.VMEM((GX, 2, GY, 128), F32)
    dma = pltpu.SemaphoreType.DMA
    out = jax.ShapeDtypeStruct(conc_old.shape, F32)
    kept = pltpu.VMEM(conc_old.shape, F32)
    hbm = pl.BlockSpec(memory_space=pl.ANY)
    vmem = pl.BlockSpec(memory_space=pltpu.VMEM)

    def faces(n, deep, dtype=F32):
        c = 8 * ((4 * deep + 7) // 8)
        return [pltpu.VMEM((2, 2, n * deep, 128), dtype), pltpu.VMEM((2, 2, n * deep + 2 * c, 128), dtype)]

    fields = pl.pallas_call(
        functools.partial(kernel, n_grp, n_dev),
        out_shape=(kept, kept, kept),
        in_specs=[hbm] * 6,
        out_specs=(vmem, vmem, vmem),
        scratch_shapes=[
            fine, pltpu.VMEM((FX, 2, FY, 128), jnp.int32), fine, pltpu.VMEM((32, 2, 32, 128), F32),
            fine, fine, pltpu.VMEM((32, 2, 32, 128), F32), fine, fine, fine, fine, fine, fine, fine, fine,
            mid, mid, mid, mid, mid, mid, mid,
            coarse, coarse, coarse, coarse, coarse, coarse, coarse, coarse, coarse, coarse,
            pltpu.VMEM((EX, 2, EY, 128), F32),
            *faces(32, 4), *faces(32, 3, jnp.int32), *faces(32, 3), *faces(32, 2), *faces(32, 2),
            *faces(16, 2), *faces(16, 2), *faces(16, 3), *faces(8, 2),
            pltpu.VMEM((2, 2, 128), jnp.int32), pltpu.VMEM((n_dev, 2, 2, 128), jnp.int32), pltpu.VMEM((64, 4096), F32),
            pltpu.VMEM((2, 128), F32), pltpu.VMEM((n_dev, 2, 128), F32), pltpu.VMEM((3, 8, 128), F32),
            dma((10,)), dma((9, 8)), dma((9, 8)), dma((2, 2)), dma((2, 2)),
            dma((n_dev,)), dma((n_dev,)), dma((n_dev,)), dma((n_dev,)), dma((2,)), dma((2,)),
        ],
        compiler_params=pltpu.CompilerParams(
            collective_id=0, has_side_effects=True, vmem_limit_bytes=50 * 1024 * 1024
        ),
    )(conc_old, phi_old, solid_pot, phase_label, iface_owner.reshape(2, 128), iface_block.reshape(2, 128))
    return pl.pallas_call(
        store,
        out_shape=(out, out, out),
        in_specs=[vmem] * 3,
        out_specs=(hbm, hbm, hbm),
        scratch_shapes=[dma((3,))],
    )(*[pltpu.with_memory_space_constraint(field, pltpu.VMEM) for field in fields])


def solution(mesh):
    split = P("grp", "dev", None)
    return jax.shard_map(
        body,
        mesh=mesh,
        in_specs=(split, split, split, split, P("grp", "dev"), split),
        out_specs=(split, split, split),
        check_vma=False,
    )
```

time: 86.6 us -> 62.1 us (0.72)
  Pallas kernels: 79.4 us -> 60.6 us
  local copies, waits for them, and re-layouts: 5.65 us -> 0.68 us
    pallas_call x1 -> x2, Pallas kernels: 79.4 us -> 60.6 us  [the longest x1 59 us: body(): pl.pallas_call(functools.partial(kernel, n_grp, n_dev), out_shape=(kept,...]
    unnamed x11 -> x4, local copies, waits for them, and re-layouts: 5.57 us -> 0.68 us
where the time goes in v2:
time: 62.1 us; the launch traced here: 62 us
  Pallas kernels  60.6 us (98%)
  local copies, waits for them, and re-layouts  0.68 us (1%)
  between operations  0.66 us (1%)
    pallas_call x1, Pallas kernels, body(): pl.pallas_call(functools.partial(kernel, n_grp, n_dev), out_shape=(kept,...  59 us
    pallas_call x1, Pallas kernels, body(): pl.pallas_call(store, out_shape=(out, out, out), in_specs=[vmem] * 3, out...  1.69 us

profile of v2, /device:TPU:1, one launch (start us, length us, event | category | flops | bytes accessed | tf_op | source)
XLA Modules:
  0.0 62.0 jit_solution(18137969718657619895)
XLA Ops:
  0.6 0.0 copy-start.1
  0.6 0.0 copy-start
  0.7 0.7 %copy-done.1 = s32[1,256]{1,0:T(1,128)S(1)} copy-done((s32[1,256]{1,0:T(1,128)S(1)}, s32[1,256]{1,0:T(1,128)}, u32[]{:S(2)}) %copy-start.1) | copy-done | bytes 1048
  1.3 0.0 copy-done
  1.3 59.0 %shard_map.85 = (f32[32,32,256]{2,1,0:T(8,128)S(1)}, f32[32,32,256]{2,1,0:T(8,128)S(1)}, f32[32,32,256]{2,1,0:T(8,128)S(1)}) custom-call(f32[32,32,256]{2,1,0:T(8,128)} %conc_hbm.1, f32[32,32,256]{2,1,0:T(8,128)} %phi_hbm.1, f32[32,32,256]{2,1,0:T(8,128)} %solid_hbm.1, s32[32,32,256]{2,1,0:T(8,128)} %label_hbm.1, s32[2,128]{1,0:T(2,128)S(1)} %bitcast.2, ...), custom_call_target="tpu_custom_call" | custom-call | tf_op jit(solution)/shard_map/pallas_call | solution.py:614
  60.3 1.7 %shard_map.86 = (f32[32,32,256]{2,1,0:T(8,128)}, f32[32,32,256]{2,1,0:T(8,128)}, f32[32,32,256]{2,1,0:T(8,128)}) custom-call(f32[32,32,256]{2,1,0:T(8,128)S(1)} %get-tuple-element.6.conc, f32[32,32,256]{2,1,0:T(8,128)S(1)} %get-tuple-element.7.flux, f32[32,32,256]{2,1,0:T(8,128)S(1)} %get-tuple-element.8.pot), custom_call_target="tpu_custom_call" | custom-call | tf_op jit(solution)/shard_map/pallas_call | solution.py:636
Async XLA Ops:
  0.6 0.7 %copy-start.1 = (s32[1,256]{1,0:T(1,128)S(1)}, s32[1,256]{1,0:T(1,128)}, u32[]{:S(2)}) copy-start(s32[1,256]{1,0:T(1,128)} %param.10) | copy-start | bytes 3076
  0.6 0.7 %copy-start = (s32[1,256,1]{1,2,0:T(1,128)S(1)}, s32[1,256,1]{1,2,0:T(1,128)}, u32[]{:S(2)}) copy-start(s32[1,256,1]{1,2,0:T(1,128)} %param.11) | copy-start | bytes 3076

commit v3 on v2

--- a/solution.py
+++ b/solution.py
@@ -18,6 +18,32 @@
 
 def lookup(label, table):
     return jnp.where(label == 0, table[0], jnp.where(label == 1, table[1], table[2])).astype(F32)
+
+
+def z_sum(a, b):
+    lane = lax.broadcasted_iota(jnp.int32, (1, 128), 1)
+    l0, l1 = lane == 0, lane == 127
+    ra, rb = pltpu.roll(a, 1, 1), pltpu.roll(b, 1, 1)
+    sa, sb = pltpu.roll(a, 127, 1), pltpu.roll(b, 127, 1)
+    zero = jnp.zeros_like(a)
+    za = jnp.where(l0, zero, ra) + jnp.where(l1, sb, sa)
+    zb = jnp.where(l0, ra, rb) + jnp.where(l1, zero, sb)
+    return za, zb
+
+
+def plane(field, x, h, r0, r1):
+    return (field[x - 1, h, r0:r1, :] + field[x + 1, h, r0:r1, :]) + (
+        field[x, h, r0 - 1 : r1 - 1, :] + field[x, h, r0 + 1 : r1 + 1, :]
+    )
+
+
+def stencil(field, x, r0, r1, weight):
+    a, b = field[x, 0, r0:r1, :], field[x, 1, r0:r1, :]
+    za, zb = z_sum(a, b)
+    pa, pb = plane(field, x, 0, r0, r1), plane(field, x, 1, r0, r1)
+    if weight != 1.0:
+        pa, pb = weight * pa, weight * pb
+    return (a, b), (pa + za, pb + zb)
 
 
 def kernel(
@@ -31,8 +57,10 @@
     block_hbm,
     conc_out,
     flux_out,
-    pot_out,
-    c0, lb, ph, sp, ca, cb, rs, dd, cc, kk, gg, qq, bb, fx, p2,
+    ca,
+    gg,
+    bb,
+    c0, lb, ph, sp, cb, cd, rs, dd, cc, kk, qq, fx, p2,
     sm, km, gm, bm, m1, m2, mu,
     kc, rc, gc, wa, wb, ka, kb, sc, ea, eb,
     ec,
@@ -45,8 +73,6 @@
     gu, gd = lax.rem(g + 1, n_grp), lax.rem(g + n_grp - 1, n_grp)
     du, dl = lax.rem(d + 1, n_dev), lax.rem(d + n_dev - 1, n_dev)
     eight = [(gd, dl), (gd, d), (gd, du), (g, dl), (g, du), (gu, dl), (gu, d), (gu, du)]
-    lane = lax.broadcasted_iota(jnp.int32, (1, 128), 1)
-    l0, l1 = lane == 0, lane == 127
 
     loads = []
     for k, (src, dst) in enumerate(((conc_hbm, c0), (label_hbm, lb), (phi_hbm, ph))):
@@ -61,7 +87,10 @@
             pltpu.make_async_copy(solid_hbm.at[:, :, pl.ds(128 * h, 128)], sp.at[:, h], in_sem.at[6 + h])
         )
     for k, src in enumerate((owner_hbm, block_hbm)):
-        loads.append(pltpu.make_async_copy(src, lists.at[k], in_sem.at[8 + k]))
+        for r in range(2):
+            loads.append(
+                pltpu.make_async_copy(src.at[:, pl.ds(128 * r, 128)], lists.at[k, r], in_sem.at[8 + 2 * k + r])
+            )
     for load in loads:
         load.start()
 
@@ -81,41 +110,42 @@
         ref[0] = jnp.zeros((2, GY, 128), F32)
         ref[GX - 1] = jnp.zeros((2, GY, 128), F32)
 
-    def pack(field, ys, n, deep):
+    def pack(field, ys, n, deep, off=0):
         def one(x, carry):
-            for s, r in ((0, 8), (1, 8 + n - deep)):
+            for s, r in ((0, 8 + off), (1, 8 + n - deep - off)):
                 for h in range(2):
                     ys[s, h, pl.ds(deep * x, deep), :] = field[4 + x, h, r : r + deep, :]
             return carry
 
         lax.fori_loop(0, n, one, 0, unroll=8)
 
-    def unpack(field, yr, n, deep, wide, zero):
+    def unpack(field, yr, n, deep, wide, zero, off=0, corners=True):
         edge_rows = 8 * ((4 * deep + 7) // 8)
 
         def one(x, carry):
-            for s, r, edge in ((0, 8 - deep, d == 0), (1, 8 + n, d == n_dev - 1)):
+            for s, r, edge in ((0, 8 - deep - off, d == 0), (1, 8 + n + off, d == n_dev - 1)):
                 for h in range(2):
                     v = yr[s, h, pl.ds(edge_rows + deep * (x - 4), deep), :]
                     field[x, h, r : r + deep, :] = jnp.where(edge, jnp.zeros_like(v), v)
             return carry
 
-        lax.fori_loop(4 - wide, 4 + n + wide, one, 0, unroll=8)
+        reach = wide if corners else 0
+        lax.fori_loop(4 - reach, 4 + n + reach, one, 0, unroll=8)
         if zero:
             @pl.when(g == 0)
             def _():
-                field[4 - wide : 4] = jnp.zeros(field.at[4 - wide : 4].shape, field.dtype)
+                field[4 - wide - off : 4 - off] = jnp.zeros(field.at[4 - wide : 4].shape, field.dtype)
 
             @pl.when(g == n_grp - 1)
             def _():
-                field[4 + n : 4 + n + wide] = jnp.zeros(field.at[4 - wide : 4].shape, field.dtype)
-
-    def halo(e, field, ys, yr, n, deep, wide):
+                field[4 + n + off : 4 + n + wide + off] = jnp.zeros(field.at[4 - wide : 4].shape, field.dtype)
+
+    def halo(e, field, ys, yr, n, deep, wide, off=0, corners=True):
         c = 8 * ((4 * deep + 7) // 8)
         m = n * deep
         own = pl.ds(8, n)
-        low, high = field.at[pl.ds(4, wide), :, own, :], field.at[pl.ds(4 + n - wide, wide), :, own, :]
-        to_low, to_high = field.at[pl.ds(4 - wide, wide), :, own, :], field.at[pl.ds(4 + n, wide), :, own, :]
+        low, high = field.at[pl.ds(4 + off, wide), :, own, :], field.at[pl.ds(4 + n - wide - off, wide), :, own, :]
+        to_low, to_high = field.at[pl.ds(4 - wide - off, wide), :, own, :], field.at[pl.ds(4 + n + off, wide), :, own, :]
         first, last, after, before = pl.ds(0, c), pl.ds(m - c, c), pl.ds(c + m, c), pl.ds(0, c)
         pairs = [
             (ys.at[0, :, first], yr.at[1, :, after]),
@@ -128,7 +158,7 @@
             (ys.at[1, :, last], yr.at[0, :, before]),
         ]
         copies = []
-        for i in (0, 2, 5, 7, 4, 3, 6, 1):
+        for i in (0, 2, 5, 7, 4, 3, 6, 1) if corners else (4, 3, 6, 1):
             src, dst = pairs[i]
             copies.append(
                 pltpu.make_async_remote_copy(
@@ -171,27 +201,6 @@
 
         lax.fori_loop(1, n_dev, one, 0)
 
-    def z_sum(a, b):
-        ra, rb = pltpu.roll(a, 1, 1), pltpu.roll(b, 1, 1)
-        sa, sb = pltpu.roll(a, 127, 1), pltpu.roll(b, 127, 1)
-        zero = jnp.zeros_like(a)
-        za = jnp.where(l0, zero, ra) + jnp.where(l1, sb, sa)
-        zb = jnp.where(l0, ra, rb) + jnp.where(l1, zero, sb)
-        return za, zb
-
-    def plane(field, x, h, r0, r1):
-        return (field[x - 1, h, r0:r1, :] + field[x + 1, h, r0:r1, :]) + (
-            field[x, h, r0 - 1 : r1 - 1, :] + field[x, h, r0 + 1 : r1 + 1, :]
-        )
-
-    def stencil(field, x, r0, r1, weight):
-        a, b = field[x, 0, r0:r1, :], field[x, 1, r0:r1, :]
-        za, zb = z_sum(a, b)
-        pa, pb = plane(field, x, 0, r0, r1), plane(field, x, 1, r0, r1)
-        if weight != 1.0:
-            pa, pb = weight * pa, weight * pb
-        return (a, b), (pa + za, pb + zb)
-
     def sweep(src, dst, gain, rhs, x0, x1, r0, r1, weight, unroll):
         def one(x, carry):
             v, s = stencil(src, x, r0, r1, weight)
@@ -233,8 +242,8 @@
     loads[4].wait()
     loads[5].wait()
     pack(ph, ysp, 32, 3)
-    loads[8].wait()
-    loads[9].wait()
+    for k in range(8, 12):
+        loads[k].wait()
     lrecv[d] = lists[...]
 
     def own_mid(i, carry):
@@ -290,6 +299,19 @@
     h_conc = halo(0, c0, ysc, yrc, 32, 4, 4)
     h_label = halo(1, lb, ysl, yrl, 32, 3, 3)
     all_send(lists, lrecv, ls_sem, lr_sem)
+
+    def conc_at(src, dst, x, r0, r1):
+        _, s = stencil(src, x, r0, r1, 1.0)
+        for h in range(2):
+            v = cc[x, h, r0:r1, :] + dd[x, h, r0:r1, :] * s[h]
+            if dst is None:
+                conc_out[x - 4, r0 - 8 : r1 - 8, 128 * h : 128 * h + 128] = v
+            else:
+                dst[x, h, r0:r1, :] = v
+
+    steps = ((c0, ca), (ca, cb), (cb, cd), (cd, None))
+    for k, (src, dst) in enumerate(steps):
+        each(5 + k, 35 - k, 15 - k, lambda x, src=src, dst=dst: conc_at(src, dst, x, 8, 40))
     for k in (6, 7):
         loads[k].wait()
     all_wait(lists, lrecv, ls_sem, lr_sem)
@@ -297,7 +319,7 @@
     def count(s, carry):
         total = carry
         for r in range(2):
-            owner, block = lrecv[s, 0, r : r + 1, :], lrecv[s, 1, r : r + 1, :]
+            owner, block = lrecv[s, 0, r], lrecv[s, 1, r]
             place = jnp.where(owner == d, (block & 1) * 32 + ((block >> 1) & 31), -1)
             column = block >> 6
             rows = (lax.broadcasted_iota(jnp.int32, (64, 128), 0) == place).astype(jnp.bfloat16)
@@ -319,42 +341,43 @@
     unpack(lb, yrl, 32, 3, 3, False)
     h_phi = halo(2, ph, ysp, yrp, 32, 3, 3)
     x_kc = coarse_exchange(kc, 0)
-    each(1, 4, 3, lambda x: conc_coeffs(x, 0, 48))
-    each(36, 39, 3, lambda x: conc_coeffs(x, 0, 48))
+    each(1, 4, 3, lambda x: conc_coeffs(x, 0, 48), lambda x: conc_coeffs(x + 35, 0, 48))
     each(4, 36, 8, lambda x: conc_coeffs(x, 0, 8), lambda x: conc_coeffs(x, 40, 48))
-
-    def conc_sweep(src, dst, x0, x1, r0, r1, unroll):
-        def one(x, carry):
-            _, s = stencil(src, x, r0, r1, 1.0)
-            for h in range(2):
-                v = cc[x, h, r0:r1, :] + dd[x, h, r0:r1, :] * s[h]
-                if dst is None:
-                    conc_out[x - 4, :, 128 * h : 128 * h + 128] = v
-                else:
-                    dst[x, h, r0:r1, :] = v
-            return carry
-
-        lax.fori_loop(x0, x1, one, 0, unroll=unroll)
-
-    conc_sweep(c0, ca, 1, 39, 4, 44, 19)
-    conc_sweep(ca, cb, 2, 38, 4, 44, 18)
-    conc_sweep(cb, ca, 3, 37, 4, 44, 17)
-    conc_sweep(ca, None, 4, 36, 8, 40, 16)
+    for k, (src, dst) in enumerate(steps):
+        r0, r1, low, high = (4, 44, (4, 12), (36, 44)) if k < 3 else (8, 40, (8, 16), (32, 40))
+        each(
+            1 + k, 5 + k, 4,
+            lambda x, src=src, dst=dst, r0=r0, r1=r1: conc_at(src, dst, x, r0, r1),
+            lambda x, src=src, dst=dst, r0=r0, r1=r1, k=k: conc_at(src, dst, x + 34 - 2 * k, r0, r1),
+        )
+        each(
+            5 + k, 35 - k, 15 - k,
+            lambda x, src=src, dst=dst, low=low: conc_at(src, dst, x, *low),
+            lambda x, src=src, dst=dst, high=high: conc_at(src, dst, x, *high),
+        )
+
+    def flux_at(x, r0, r1):
+        for h in range(2):
+            con = conc_out[x, r0:r1, 128 * h : 128 * h + 128]
+            u = 0.5 * (sp[x, h, r0:r1, :] - ph[4 + x, h, 8 + r0 : 8 + r1, :]) - 0.1 * jnp.log(con)
+            kin = lookup(lb[4 + x, h, 8 + r0 : 8 + r1, :], (0.2, 1.0, 0.5)) * jnp.sqrt(con)
+            val = kin * (jnp.exp(u) - jnp.exp(-u))
+            val = msk[32 * h + r0 : 32 * h + r1, 128 * x : 128 * x + 128] * val
+            fx[4 + x, h, 8 + r0 : 8 + r1, :] = val
+            flux_out[x, r0:r1, 128 * h : 128 * h + 128] = val
 
     for x in range(32):
-        for h in range(2):
-            con = conc_out[x, :, 128 * h : 128 * h + 128]
-            u = 0.5 * (sp[x, h] - ph[4 + x, h, 8:40, :]) - 0.1 * jnp.log(con)
-            kin = lookup(lb[4 + x, h, 8:40, :], (0.2, 1.0, 0.5)) * jnp.sqrt(con)
-            val = kin * (jnp.exp(u) - jnp.exp(-u))
-            val = msk[32 * h : 32 * h + 32, 128 * x : 128 * x + 128] * val
-            fx[4 + x, h, 8:40, :] = val
-            flux_out[x, :, 128 * h : 128 * h + 128] = val
+        if x in (0, 1, 30, 31):
+            flux_at(x, 0, 32)
+        else:
+            flux_at(x, 0, 8)
+            flux_at(x, 24, 32)
     pack(fx, ysf, 32, 2)
     h_flux = halo(4, fx, ysf, yrf, 32, 2, 2)
-
-    each(2, 4, 2, lambda x: pot_coeffs(x, 0, 48))
-    each(36, 38, 2, lambda x: pot_coeffs(x, 0, 48))
+    for x in range(2, 30):
+        flux_at(x, 8, 24)
+
+    each(2, 4, 2, lambda x: pot_coeffs(x, 0, 48), lambda x: pot_coeffs(x + 34, 0, 48))
     each(4, 36, 8, lambda x: pot_coeffs(x, 0, 8), lambda x: pot_coeffs(x, 40, 48))
     arrive(h_phi)
     unpack(ph, yrp, 32, 3, 3, True)
@@ -367,6 +390,31 @@
         return carry
 
     lax.fori_loop(2, 38, first, 0, unroll=12)
+
+    def second(x, r0, r1):
+        for h in range(2):
+            rd = bb[x, h, r0:r1, :]
+            fl = fx[x, h, r0:r1, :]
+            ca[x, h, r0:r1, :] = qq[x, h, r0:r1, :] + rd * fl
+            src = 0.05 * ph[x, h, r0:r1, :] + fl
+            qq[x, h, r0:r1, :] = src
+            bb[x, h, r0:r1, :] = rd * src
+
+    def smooth(x, r0, r1):
+        v, s = stencil(ca, x, r0, r1, 1.0)
+        for h in range(2):
+            p2[x, h, r0:r1, :] = 0.2 * v[h] + bb[x, h, r0:r1, :] + gg[x, h, r0:r1, :] * s[h]
+
+    def resid(x, r0, r1):
+        v, s = stencil(p2, x, r0, r1, 1.0)
+        for h in range(2):
+            rs[x - 4, h, r0 - 8 : r1 - 8, :] = (
+                qq[x, h, r0:r1, :] - 0.05 * v[h] - kk[x, h, r0:r1, :] * (6.0 * v[h] - s[h])
+            )
+
+    each(4, 36, 8, lambda x: second(x, 8, 40))
+    each(5, 35, 15, lambda x: smooth(x, 8, 40))
+    each(6, 34, 14, lambda x: resid(x, 8, 40))
     arrive(x_kc)
     coarse_edges(kc)
 
@@ -413,27 +461,12 @@
     arrive(h_flux)
     unpack(fx, yrf, 32, 2, 2, True)
     h_km = halo(3, km, ysk, yrk, 16, 2, 2)
-
-    def second(x, carry):
-        for h in range(2):
-            rd = bb[x, h, 4:44, :]
-            fl = fx[x, h, 4:44, :]
-            ca[x, h, 4:44, :] = qq[x, h, 4:44, :] + rd * fl
-            src = 0.05 * ph[x, h, 4:44, :] + fl
-            qq[x, h, 4:44, :] = src
-            bb[x, h, 4:44, :] = rd * src
-        return carry
-
-    lax.fori_loop(2, 38, second, 0, unroll=6)
-    sweep(ca, p2, gg, bb, 3, 37, 4, 44, 1.0, 17)
-
-    def resid(x, carry):
-        v, s = stencil(p2, x, 8, 40, 1.0)
-        for h in range(2):
-            rs[x - 4, h] = qq[x, h, 8:40, :] - 0.05 * v[h] - kk[x, h, 8:40, :] * (6.0 * v[h] - s[h])
-        return carry
-
-    lax.fori_loop(4, 36, resid, 0, unroll=16)
+    each(2, 4, 2, lambda x: second(x, 4, 44), lambda x: second(x + 34, 4, 44))
+    each(4, 36, 8, lambda x: second(x, 0, 8), lambda x: second(x, 40, 48))
+    each(3, 5, 2, lambda x: smooth(x, 4, 44), lambda x: smooth(x + 32, 4, 44))
+    each(5, 35, 15, lambda x: smooth(x, 4, 12), lambda x: smooth(x, 36, 44))
+    each(4, 6, 2, lambda x: resid(x, 8, 40), lambda x: resid(x + 30, 8, 40))
+    each(6, 34, 14, lambda x: resid(x, 8, 16), lambda x: resid(x, 32, 40))
 
     def down(i, carry):
         for h in range(2):
@@ -447,7 +480,7 @@
     lax.fori_loop(0, 16, down, 0, unroll=8)
     pack(sm, yss, 16, 2)
     h_sm = halo(5, sm, yss, yrs, 16, 2, 2)
-    pack(p2, ysu, 32, 2)
+    pack(p2, ysu, 32, 1, 1)
     arrive(h_km)
     unpack(km, yrk, 16, 2, 2, True)
 
@@ -460,9 +493,9 @@
         return carry
 
     lax.fori_loop(2, 22, mid_coeffs, 0, unroll=5)
+    h_p2 = halo(7, p2, ysu, yru, 32, 1, 1, 1, False)
     arrive(h_sm)
     unpack(sm, yrs, 16, 2, 2, True)
-    h_p2 = halo(7, p2, ysu, yru, 32, 2, 2)
 
     def mid_first(x, carry):
         for h in range(2):
@@ -495,9 +528,9 @@
     precv[d] = message
     all_send(psend, precv, ps_sem, pr_sem)
     pack(mu, ysm, 16, 3)
-    h_mu = halo(8, mu, ysm, yrm, 16, 3, 3)
     arrive(x_sc)
     coarse_edges(sc)
+    h_mu = halo(8, mu, ysm, yrm, 16, 3, 3)
 
     def coarse_first(x, carry):
         for h in range(2):
@@ -539,7 +572,7 @@
     unpack(mu, yrm, 16, 3, 3, True)
     arrive(h_p2)
     sent(h_p2)
-    unpack(p2, yru, 32, 2, 2, True)
+    unpack(p2, yru, 32, 1, 1, True, 1, False)
     arrive(h_ec)
     unpack(ec, yre, 8, 2, 2, True)
     arrive(x_shift)
@@ -573,25 +606,27 @@
     lax.fori_loop(3, 21, fine_up, 0, unroll=6)
     sweep(p2, ca, gg, bb, 3, 37, 4, 44, 1.0, 17)
 
-    def last(x, carry):
-        v, s = stencil(ca, x, 8, 40, 1.0)
-        for h in range(2):
-            new = 0.2 * v[h] + bb[x, h, 8:40, :] + gg[x, h, 8:40, :] * s[h]
-            pot_out[x - 4, :, 128 * h : 128 * h + 128] = new
-        return carry
-
-    lax.fori_loop(4, 36, last, 0, unroll=16)
     for copies in (h_conc, h_label, h_phi, h_km, h_flux, h_sm, h_ec, x_kc, x_sc, x_shift):
         sent(copies)
 
 
-def store(conc, flux, pot, conc_out, flux_out, pot_out, sem):
-    copies = [
-        pltpu.make_async_copy(src, dst, sem.at[k])
-        for k, (src, dst) in enumerate(((conc, conc_out), (flux, flux_out), (pot, pot_out)))
-    ]
+def finish(conc, flux, last, gain, rhs, conc_out, flux_out, pot_out, pot, sem):
+    copies = [pltpu.make_async_copy(conc, conc_out, sem.at[4]), pltpu.make_async_copy(flux, flux_out, sem.at[5])]
     for c in copies:
         c.start()
+
+    def one(x, carry):
+        v, s = stencil(last, x, 8, 40, 1.0)
+        for h in range(2):
+            new = 0.2 * v[h] + rhs[x, h, 8:40, :] + gain[x, h, 8:40, :] * s[h]
+            pot[x - 4, :, 128 * h : 128 * h + 128] = new
+        return carry
+
+    for k in range(4):
+        lax.fori_loop(4 + 8 * k, 12 + 8 * k, one, 0, unroll=8)
+        part = pl.ds(8 * k, 8)
+        copies.append(pltpu.make_async_copy(pot.at[part], pot_out.at[part], sem.at[k]))
+        copies[-1].start()
     for c in copies:
         c.wait()
 
@@ -604,41 +639,43 @@
     dma = pltpu.SemaphoreType.DMA
     out = jax.ShapeDtypeStruct(conc_old.shape, F32)
     kept = pltpu.VMEM(conc_old.shape, F32)
-    hbm = pl.BlockSpec(memory_space=pl.ANY)
+    hbm = pl.BlockSpec(memory_space=pltpu.HBM)
     vmem = pl.BlockSpec(memory_space=pltpu.VMEM)
 
     def faces(n, deep, dtype=F32):
         c = 8 * ((4 * deep + 7) // 8)
         return [pltpu.VMEM((2, 2, n * deep, 128), dtype), pltpu.VMEM((2, 2, n * deep + 2 * c, 128), dtype)]
 
+    arguments = (conc_old, phi_old, solid_pot, phase_label, iface_owner.reshape(1, 256), iface_block)
     fields = pl.pallas_call(
         functools.partial(kernel, n_grp, n_dev),
-        out_shape=(kept, kept, kept),
+        out_shape=(kept, kept, fine, fine, fine),
         in_specs=[hbm] * 6,
-        out_specs=(vmem, vmem, vmem),
+        out_specs=(vmem,) * 5,
         scratch_shapes=[
             fine, pltpu.VMEM((FX, 2, FY, 128), jnp.int32), fine, pltpu.VMEM((32, 2, 32, 128), F32),
-            fine, fine, pltpu.VMEM((32, 2, 32, 128), F32), fine, fine, fine, fine, fine, fine, fine, fine,
+            fine, fine, pltpu.VMEM((32, 2, 32, 128), F32), fine, fine, fine, fine, fine, fine,
             mid, mid, mid, mid, mid, mid, mid,
             coarse, coarse, coarse, coarse, coarse, coarse, coarse, coarse, coarse, coarse,
             pltpu.VMEM((EX, 2, EY, 128), F32),
-            *faces(32, 4), *faces(32, 3, jnp.int32), *faces(32, 3), *faces(32, 2), *faces(32, 2),
+            *faces(32, 4), *faces(32, 3, jnp.int32), *faces(32, 3), *faces(32, 2), *faces(32, 1),
             *faces(16, 2), *faces(16, 2), *faces(16, 3), *faces(8, 2),
-            pltpu.VMEM((2, 2, 128), jnp.int32), pltpu.VMEM((n_dev, 2, 2, 128), jnp.int32), pltpu.VMEM((64, 4096), F32),
+            pltpu.VMEM((2, 2, 1, 128), jnp.int32), pltpu.VMEM((n_dev, 2, 2, 1, 128), jnp.int32), pltpu.VMEM((64, 4096), F32),
             pltpu.VMEM((2, 128), F32), pltpu.VMEM((n_dev, 2, 128), F32), pltpu.VMEM((3, 8, 128), F32),
-            dma((10,)), dma((9, 8)), dma((9, 8)), dma((2, 2)), dma((2, 2)),
+            dma((12,)), dma((9, 8)), dma((9, 8)), dma((2, 2)), dma((2, 2)),
             dma((n_dev,)), dma((n_dev,)), dma((n_dev,)), dma((n_dev,)), dma((2,)), dma((2,)),
         ],
         compiler_params=pltpu.CompilerParams(
-            collective_id=0, has_side_effects=True, vmem_limit_bytes=50 * 1024 * 1024
+            collective_id=0, has_side_effects=True, vmem_limit_bytes=43 * 1024 * 1024
         ),
-    )(conc_old, phi_old, solid_pot, phase_label, iface_owner.reshape(2, 128), iface_block.reshape(2, 128))
+    )(*[pltpu.with_memory_space_constraint(argument, pltpu.HBM) for argument in arguments])
     return pl.pallas_call(
-        store,
+        finish,
         out_shape=(out, out, out),
-        in_specs=[vmem] * 3,
+        in_specs=[vmem] * 5,
         out_specs=(hbm, hbm, hbm),
-        scratch_shapes=[dma((3,))],
+        scratch_shapes=[pltpu.VMEM(conc_old.shape, F32), dma((6,))],
+        compiler_params=pltpu.CompilerParams(vmem_limit_bytes=8 * 1024 * 1024),
     )(*[pltpu.with_memory_space_constraint(field, pltpu.VMEM) for field in fields])
 
 

time: 62.1 us -> 59.2 us (0.953)
  Pallas kernels: 60.6 us -> 58.5 us
  local copies, waits for them, and re-layouts: 0.68 us -> 0 us
    pallas_call x1, Pallas kernels: 59 us -> 56.8 us  [body(): pl.pallas_call(functools.partial(kernel, n_grp, n_dev), out_shape=(kept,...]
    unnamed x4 -> x0, local copies, waits for them, and re-layouts: 0.68 us -> none
where the time goes in v3:
time: 59.2 us; the launch traced here: 59.1 us
  Pallas kernels  58.5 us (99%)
  between operations  0.64 us (1%)
    pallas_call x1, Pallas kernels, body(): pl.pallas_call(functools.partial(kernel, n_grp, n_dev), out_shape=(kept,...  56.8 us
    pallas_call x1, Pallas kernels, body(): pl.pallas_call(finish, out_shape=(out, out, out), in_specs=[vmem] * 5, ou...  1.71 us

profile of v3, /device:TPU:1, one launch (start us, length us, event | category | flops | bytes accessed | tf_op | source)
XLA Modules:
  0.0 59.1 jit_solution(15404390086646279181)
XLA Ops:
  0.6 56.8 %shard_map.85 = (f32[32,32,256]{2,1,0:T(8,128)S(1)}, f32[32,32,256]{2,1,0:T(8,128)S(1)}, f32[40,2,48,128]{3,2,1,0:T(8,128)S(1)}, f32[40,2,48,128]{3,2,1,0:T(8,128)S(1)}, f32[40,2,48,128]{3,2,1,0:T(8,128)S(1)}) custom-call(f32[32,32,256]{2,1,0:T(8,128)} %conc_hbm.1, f32[32,32,256]{2,1,0:T(8,128)} %phi_hbm.1, f32[32,32,256]{2,1,0:T(8,128)} %solid_hbm.1, ...), custom_call_target="tpu_custom_call" | custom-call | tf_op jit(solution)/shard_map/pallas_call | solution.py:650
  57.4 1.7 %shard_map.86 = (f32[32,32,256]{2,1,0:T(8,128)}, f32[32,32,256]{2,1,0:T(8,128)}, f32[32,32,256]{2,1,0:T(8,128)}) custom-call(f32[32,32,256]{2,1,0:T(8,128)S(1)} %get-tuple-element.8.conc, f32[32,32,256]{2,1,0:T(8,128)S(1)} %get-tuple-element.9.flux, f32[40,2,48,128]{3,2,1,0:T(8,128)S(1)} %get-tuple-element.10.last, ...), custom_call_target="tpu_custom_call" | custom-call | tf_op jit(solution)/shard_map/pallas_call | solution.py:672

commit v4 on v3

--- a/solution.py
+++ b/solution.py
@@ -65,7 +65,7 @@
     kc, rc, gc, wa, wb, ka, kb, sc, ea, eb,
     ec,
     ysc, yrc, ysl, yrl, ysp, yrp, ysf, yrf, ysu, yru, ysk, yrk, yss, yrs, ysm, yrm, yse, yre,
-    lists, lrecv, msk, psend, precv, shifts,
+    lists, lsend, lrecv, msk, psend, precv, shifts,
     in_sem, hs_sem, hr_sem, cs_sem, cr_sem, ls_sem, lr_sem, ps_sem, pr_sem, ss_sem, sr_sem,
 ):
     g = lax.axis_index("grp")
@@ -181,7 +181,7 @@
     def all_send(src, dst, send_sem, recv_sem):
         def one(j, carry):
             pltpu.make_async_remote_copy(
-                src_ref=src, dst_ref=dst.at[d], send_sem=send_sem.at[j], recv_sem=recv_sem.at[d],
+                src_ref=src.at[lax.rem(d + j, n_dev)] if src.shape[0] == n_dev else src, dst_ref=dst.at[d], send_sem=send_sem.at[j], recv_sem=recv_sem.at[d],
                 device_id=(g, lax.rem(d + j, n_dev)), device_id_type=MESH,
             ).start()
             return carry
@@ -192,7 +192,7 @@
         def one(j, carry):
             s = lax.rem(d + n_dev - j, n_dev)
             c = pltpu.make_async_remote_copy(
-                src_ref=src, dst_ref=dst.at[s], send_sem=send_sem.at[j], recv_sem=recv_sem.at[s],
+                src_ref=src.at[lax.rem(d + j, n_dev)] if src.shape[0] == n_dev else src, dst_ref=dst.at[s], send_sem=send_sem.at[j], recv_sem=recv_sem.at[s],
                 device_id=(g, lax.rem(d + j, n_dev)), device_id_type=MESH,
             )
             c.wait_recv()
@@ -244,7 +244,27 @@
     pack(ph, ysp, 32, 3)
     for k in range(8, 12):
         loads[k].wait()
-    lrecv[d] = lists[...]
+    owners = jnp.concatenate([lists[0, 0], lists[0, 1]], axis=1)
+    values = jnp.concatenate([lists[1, 0], lists[1, 1]], axis=1) + 1
+    onehot = lax.broadcasted_iota(jnp.int32, (n_dev, 256), 0) == owners
+    ones = jnp.where(onehot, 1.0, 0.0)
+    earlier = lax.broadcasted_iota(jnp.int32, (256, 256), 0) < lax.broadcasted_iota(jnp.int32, (256, 256), 1)
+    before = jnp.dot(
+        ones.astype(jnp.bfloat16), jnp.where(earlier, 1.0, 0.0).astype(jnp.bfloat16), preferred_element_type=F32
+    )
+    rank = jnp.sum(ones * before, axis=0, keepdims=True) + (16 * lax.rem(d, 8)).astype(F32)
+    slots = lax.broadcasted_iota(jnp.int32, (128, 256), 0).astype(F32) == rank
+    slots = jnp.where(slots, 1.0, 0.0).astype(jnp.bfloat16)
+    by_owner = jnp.zeros((n_dev, 128), F32)
+    for part, scale in ((values >> 6, 64.0), (values & 63, 1.0)):
+        terms = jnp.where(onehot, part.astype(F32), 0.0).astype(jnp.bfloat16)
+        by_owner = by_owner + scale * lax.dot_general(
+            terms, slots, (((1,), (1,)), ((), ())), preferred_element_type=F32
+        )
+    by_owner = by_owner.astype(jnp.int32) - 1
+    for o in range(n_dev):
+        lsend[o] = by_owner[o : o + 1, :]
+    lrecv[d] = lsend[d]
 
     def own_mid(i, carry):
         for h in range(2):
@@ -296,9 +316,9 @@
     own_coarse(kc, km, 4)
 
     pl.semaphore_wait(barrier, n_dev - 1 + 6)
+    all_send(lsend, lrecv, ls_sem, lr_sem)
     h_conc = halo(0, c0, ysc, yrc, 32, 4, 4)
     h_label = halo(1, lb, ysl, yrl, 32, 3, 3)
-    all_send(lists, lrecv, ls_sem, lr_sem)
 
     def conc_at(src, dst, x, r0, r1):
         _, s = stencil(src, x, r0, r1, 1.0)
@@ -314,22 +334,17 @@
         each(5 + k, 35 - k, 15 - k, lambda x, src=src, dst=dst: conc_at(src, dst, x, 8, 40))
     for k in (6, 7):
         loads[k].wait()
-    all_wait(lists, lrecv, ls_sem, lr_sem)
-
-    def count(s, carry):
-        total = carry
-        for r in range(2):
-            owner, block = lrecv[s, 0, r], lrecv[s, 1, r]
-            place = jnp.where(owner == d, (block & 1) * 32 + ((block >> 1) & 31), -1)
-            column = block >> 6
-            rows = (lax.broadcasted_iota(jnp.int32, (64, 128), 0) == place).astype(jnp.bfloat16)
-            cols = (lax.broadcasted_iota(jnp.int32, (32, 128), 0) == column).astype(jnp.bfloat16)
-            total = total + lax.dot_general(
-                rows, cols, (((1,), (1,)), ((), ())), preferred_element_type=F32
-            )
-        return total
-
-    counts = lax.fori_loop(0, n_dev, count, jnp.zeros((64, 32), F32), unroll=8)
+    all_wait(lsend, lrecv, ls_sem, lr_sem)
+
+    counts = jnp.zeros((64, 32), F32)
+    for q in range(n_dev // 8):
+        block = lrecv[8 * q]
+        for k in range(1, 8):
+            block = jnp.maximum(block, lrecv[8 * q + k])
+        place = jnp.where(block >= 0, (block & 1) * 32 + ((block >> 1) & 31), -1)
+        rows = jnp.where(lax.broadcasted_iota(jnp.int32, (64, 128), 0) == place, 1.0, 0.0).astype(jnp.bfloat16)
+        cols = jnp.where(lax.broadcasted_iota(jnp.int32, (32, 128), 0) == block >> 6, 1.0, 0.0).astype(jnp.bfloat16)
+        counts = counts + lax.dot_general(rows, cols, (((1,), (1,)), ((), ())), preferred_element_type=F32)
     named = jnp.where(counts > 0.0, 1.0, 0.0).astype(jnp.bfloat16)
     spread = (
         lax.broadcasted_iota(jnp.int32, (32, 4096), 1) // 128 == lax.broadcasted_iota(jnp.int32, (32, 4096), 0)
@@ -340,7 +355,6 @@
     arrive(h_label)
     unpack(lb, yrl, 32, 3, 3, False)
     h_phi = halo(2, ph, ysp, yrp, 32, 3, 3)
-    x_kc = coarse_exchange(kc, 0)
     each(1, 4, 3, lambda x: conc_coeffs(x, 0, 48), lambda x: conc_coeffs(x + 35, 0, 48))
     each(4, 36, 8, lambda x: conc_coeffs(x, 0, 8), lambda x: conc_coeffs(x, 40, 48))
     for k, (src, dst) in enumerate(steps):
@@ -415,6 +429,43 @@
     each(4, 36, 8, lambda x: second(x, 8, 40))
     each(5, 35, 15, lambda x: smooth(x, 8, 40))
     each(6, 34, 14, lambda x: resid(x, 8, 40))
+    arrive(h_flux)
+    unpack(fx, yrf, 32, 2, 2, True)
+    h_km = halo(3, km, ysk, yrk, 16, 2, 2)
+    x_kc = coarse_exchange(kc, 0)
+    each(2, 4, 2, lambda x: second(x, 4, 44), lambda x: second(x + 34, 4, 44))
+    each(4, 36, 8, lambda x: second(x, 0, 8), lambda x: second(x, 40, 48))
+    each(3, 5, 2, lambda x: smooth(x, 4, 44), lambda x: smooth(x + 32, 4, 44))
+    each(5, 35, 15, lambda x: smooth(x, 4, 12), lambda x: smooth(x, 36, 44))
+    each(4, 6, 2, lambda x: resid(x, 8, 40), lambda x: resid(x + 30, 8, 40))
+    each(6, 34, 14, lambda x: resid(x, 8, 16), lambda x: resid(x, 32, 40))
+
+    def down(i, carry):
+        for h in range(2):
+            total = jnp.zeros((16, 128), F32)
+            for x in (0, 1):
+                for r in (0, 1):
+                    total = total + rs[2 * i + x, h, pl.ds(r, 16, stride=2), :]
+            sm[4 + i, h, 8:24, :] = 0.25 * total
+        return carry
+
+    lax.fori_loop(0, 16, down, 0, unroll=8)
+    pack(sm, yss, 16, 2)
+    h_sm = halo(5, sm, yss, yrs, 16, 2, 2)
+    pack(p2, ysu, 32, 1, 1)
+    arrive(h_km)
+    unpack(km, yrk, 16, 2, 2, True)
+
+    def mid_coeffs(x, carry):
+        for h in range(2):
+            con = km[x, h, 4:28, :]
+            rd = 0.8 / (0.05 + 3.0 * con)
+            bm[x, h, 4:28, :] = rd
+            gm[x, h, 4:28, :] = rd * con
+        return carry
+
+    lax.fori_loop(2, 22, mid_coeffs, 0, unroll=5)
+    h_p2 = halo(7, p2, ysu, yru, 32, 1, 1, 1, False)
     arrive(x_kc)
     coarse_edges(kc)
 
@@ -458,42 +509,6 @@
     load = jnp.sum(load, axis=0, keepdims=True)
     row2 = lax.broadcasted_iota(jnp.int32, (2, 128), 0)
 
-    arrive(h_flux)
-    unpack(fx, yrf, 32, 2, 2, True)
-    h_km = halo(3, km, ysk, yrk, 16, 2, 2)
-    each(2, 4, 2, lambda x: second(x, 4, 44), lambda x: second(x + 34, 4, 44))
-    each(4, 36, 8, lambda x: second(x, 0, 8), lambda x: second(x, 40, 48))
-    each(3, 5, 2, lambda x: smooth(x, 4, 44), lambda x: smooth(x + 32, 4, 44))
-    each(5, 35, 15, lambda x: smooth(x, 4, 12), lambda x: smooth(x, 36, 44))
-    each(4, 6, 2, lambda x: resid(x, 8, 40), lambda x: resid(x + 30, 8, 40))
-    each(6, 34, 14, lambda x: resid(x, 8, 16), lambda x: resid(x, 32, 40))
-
-    def down(i, carry):
-        for h in range(2):
-            total = jnp.zeros((16, 128), F32)
-            for x in (0, 1):
-                for r in (0, 1):
-                    total = total + rs[2 * i + x, h, pl.ds(r, 16, stride=2), :]
-            sm[4 + i, h, 8:24, :] = 0.25 * total
-        return carry
-
-    lax.fori_loop(0, 16, down, 0, unroll=8)
-    pack(sm, yss, 16, 2)
-    h_sm = halo(5, sm, yss, yrs, 16, 2, 2)
-    pack(p2, ysu, 32, 1, 1)
-    arrive(h_km)
-    unpack(km, yrk, 16, 2, 2, True)
-
-    def mid_coeffs(x, carry):
-        for h in range(2):
-            con = km[x, h, 4:28, :]
-            rd = 0.8 / (0.05 + 3.0 * con)
-            bm[x, h, 4:28, :] = rd
-            gm[x, h, 4:28, :] = rd * con
-        return carry
-
-    lax.fori_loop(2, 22, mid_coeffs, 0, unroll=5)
-    h_p2 = halo(7, p2, ysu, yru, 32, 1, 1, 1, False)
     arrive(h_sm)
     unpack(sm, yrs, 16, 2, 2, True)
 
@@ -660,7 +675,7 @@
             pltpu.VMEM((EX, 2, EY, 128), F32),
             *faces(32, 4), *faces(32, 3, jnp.int32), *faces(32, 3), *faces(32, 2), *faces(32, 1),
             *faces(16, 2), *faces(16, 2), *faces(16, 3), *faces(8, 2),
-            pltpu.VMEM((2, 2, 1, 128), jnp.int32), pltpu.VMEM((n_dev, 2, 2, 1, 128), jnp.int32), pltpu.VMEM((64, 4096), F32),
+            pltpu.VMEM((2, 2, 1, 128), jnp.int32), pltpu.VMEM((n_dev, 1, 128), jnp.int32), pltpu.VMEM((n_dev, 1, 128), jnp.int32), pltpu.VMEM((64, 4096), F32),
             pltpu.VMEM((2, 128), F32), pltpu.VMEM((n_dev, 2, 128), F32), pltpu.VMEM((3, 8, 128), F32),
             dma((12,)), dma((9, 8)), dma((9, 8)), dma((2, 2)), dma((2, 2)),
             dma((n_dev,)), dma((n_dev,)), dma((n_dev,)), dma((n_dev,)), dma((2,)), dma((2,)),

time: 59.2 us -> 55 us (0.929)
  Pallas kernels: 58.5 us -> 54.2 us
    pallas_call x1, Pallas kernels: 56.8 us -> 52.5 us  [body(): pl.pallas_call(functools.partial(kernel, n_grp, n_dev), out_shape=(kept,...]
where the time goes in v4:
time: 55 us; the launch traced here: 54.9 us
  Pallas kernels  54.2 us (99%)
  between operations  0.64 us (1%)
    pallas_call x1, Pallas kernels, body(): pl.pallas_call(functools.partial(kernel, n_grp, n_dev), out_shape=(kept,...  52.5 us
    pallas_call x1, Pallas kernels, body(): pl.pallas_call(finish, out_shape=(out, out, out), in_specs=[vmem] * 5, ou...  1.71 us

profile of v4, /device:TPU:1, one launch (start us, length us, event | category | flops | bytes accessed | tf_op | source)
XLA Modules:
  0.0 54.9 jit_solution(1917776409075492099)
XLA Ops:
  0.6 52.5 %shard_map.85 = (f32[32,32,256]{2,1,0:T(8,128)S(1)}, f32[32,32,256]{2,1,0:T(8,128)S(1)}, f32[40,2,48,128]{3,2,1,0:T(8,128)S(1)}, f32[40,2,48,128]{3,2,1,0:T(8,128)S(1)}, f32[40,2,48,128]{3,2,1,0:T(8,128)S(1)}) custom-call(f32[32,32,256]{2,1,0:T(8,128)} %conc_hbm.1, f32[32,32,256]{2,1,0:T(8,128)} %phi_hbm.1, f32[32,32,256]{2,1,0:T(8,128)} %solid_hbm.1, ...), custom_call_target="tpu_custom_call" | custom-call | tf_op jit(solution)/shard_map/pallas_call | solution.py:665
  53.2 1.7 %shard_map.86 = (f32[32,32,256]{2,1,0:T(8,128)}, f32[32,32,256]{2,1,0:T(8,128)}, f32[32,32,256]{2,1,0:T(8,128)}) custom-call(f32[32,32,256]{2,1,0:T(8,128)S(1)} %get-tuple-element.8.conc, f32[32,32,256]{2,1,0:T(8,128)S(1)} %get-tuple-element.9.flux, f32[40,2,48,128]{3,2,1,0:T(8,128)S(1)} %get-tuple-element.10.last, ...), custom_call_target="tpu_custom_call" | custom-call | tf_op jit(solution)/shard_map/pallas_call | solution.py:687

commit v5 on v4

--- a/solution.py
+++ b/solution.py
@@ -356,7 +356,7 @@
     unpack(lb, yrl, 32, 3, 3, False)
     h_phi = halo(2, ph, ysp, yrp, 32, 3, 3)
     each(1, 4, 3, lambda x: conc_coeffs(x, 0, 48), lambda x: conc_coeffs(x + 35, 0, 48))
-    each(4, 36, 8, lambda x: conc_coeffs(x, 0, 8), lambda x: conc_coeffs(x, 40, 48))
+    each(4, 36, 32, lambda x: conc_coeffs(x, 0, 8), lambda x: conc_coeffs(x, 40, 48))
     for k, (src, dst) in enumerate(steps):
         r0, r1, low, high = (4, 44, (4, 12), (36, 44)) if k < 3 else (8, 40, (8, 16), (32, 40))
         each(
@@ -365,7 +365,7 @@
             lambda x, src=src, dst=dst, r0=r0, r1=r1, k=k: conc_at(src, dst, x + 34 - 2 * k, r0, r1),
         )
         each(
-            5 + k, 35 - k, 15 - k,
+            5 + k, 35 - k, 30 - 2 * k,
             lambda x, src=src, dst=dst, low=low: conc_at(src, dst, x, *low),
             lambda x, src=src, dst=dst, high=high: conc_at(src, dst, x, *high),
         )
@@ -429,16 +429,16 @@
     each(4, 36, 8, lambda x: second(x, 8, 40))
     each(5, 35, 15, lambda x: smooth(x, 8, 40))
     each(6, 34, 14, lambda x: resid(x, 8, 40))
+    h_km = halo(3, km, ysk, yrk, 16, 2, 2)
+    x_kc = coarse_exchange(kc, 0)
     arrive(h_flux)
     unpack(fx, yrf, 32, 2, 2, True)
-    h_km = halo(3, km, ysk, yrk, 16, 2, 2)
-    x_kc = coarse_exchange(kc, 0)
     each(2, 4, 2, lambda x: second(x, 4, 44), lambda x: second(x + 34, 4, 44))
-    each(4, 36, 8, lambda x: second(x, 0, 8), lambda x: second(x, 40, 48))
+    each(4, 36, 32, lambda x: second(x, 0, 8), lambda x: second(x, 40, 48))
     each(3, 5, 2, lambda x: smooth(x, 4, 44), lambda x: smooth(x + 32, 4, 44))
-    each(5, 35, 15, lambda x: smooth(x, 4, 12), lambda x: smooth(x, 36, 44))
+    each(5, 35, 30, lambda x: smooth(x, 4, 12), lambda x: smooth(x, 36, 44))
     each(4, 6, 2, lambda x: resid(x, 8, 40), lambda x: resid(x + 30, 8, 40))
-    each(6, 34, 14, lambda x: resid(x, 8, 16), lambda x: resid(x, 32, 40))
+    each(6, 34, 28, lambda x: resid(x, 8, 16), lambda x: resid(x, 32, 40))
 
     def down(i, carry):
         for h in range(2):
@@ -449,7 +449,7 @@
             sm[4 + i, h, 8:24, :] = 0.25 * total
         return carry
 
-    lax.fori_loop(0, 16, down, 0, unroll=8)
+    lax.fori_loop(0, 16, down, 0, unroll=16)
     pack(sm, yss, 16, 2)
     h_sm = halo(5, sm, yss, yrs, 16, 2, 2)
     pack(p2, ysu, 32, 1, 1)
@@ -519,7 +519,7 @@
             m1[x, h, 4:28, :] = v
         return carry
 
-    lax.fori_loop(2, 22, mid_first, 0, unroll=10)
+    lax.fori_loop(2, 22, mid_first, 0, unroll=20)
     sweep(m1, m2, gm, bm, 3, 21, 4, 28, 0.25, 18)
 
     def mid_resid(x, carry):
@@ -606,7 +606,7 @@
                 for r in (0, 1):
                     rows = pl.ds(4 + r, 12, stride=2)
                     mu[2 * i - 4 + x, h, rows, :] = mu[2 * i - 4 + x, h, rows, :] + v
-    sweep(mu, m1, gm, bm, 2, 22, 4, 28, 0.25, 10)
+    sweep(mu, m1, gm, bm, 2, 22, 4, 28, 0.25, 20)
     sweep(m1, m2, gm, bm, 3, 21, 4, 28, 0.25, 18)
 
     def fine_up(i, carry):
@@ -618,8 +618,8 @@
                     p2[2 * i - 4 + x, h, rows, :] = p2[2 * i - 4 + x, h, rows, :] + v
         return carry
 
-    lax.fori_loop(3, 21, fine_up, 0, unroll=6)
-    sweep(p2, ca, gg, bb, 3, 37, 4, 44, 1.0, 17)
+    lax.fori_loop(3, 21, fine_up, 0, unroll=18)
+    sweep(p2, ca, gg, bb, 3, 37, 4, 44, 1.0, 34)
 
     for copies in (h_conc, h_label, h_phi, h_km, h_flux, h_sm, h_ec, x_kc, x_sc, x_shift):
         sent(copies)

time: 55 us -> 54.4 us (0.989)
  Pallas kernels: 54.2 us -> 53.5 us
    pallas_call x1, Pallas kernels: 52.5 us -> 51.8 us  [body(): pl.pallas_call(functools.partial(kernel, n_grp, n_dev), out_shape=(kept,...]
where the time goes in v5:
time: 54.4 us; the launch traced here: 54.3 us
  Pallas kernels  53.5 us (98%)
  between operations  0.8 us (1%)
    pallas_call x1, Pallas kernels, body(): pl.pallas_call(functools.partial(kernel, n_grp, n_dev), out_shape=(kept,...  51.8 us
    pallas_call x1, Pallas kernels, body(): pl.pallas_call(finish, out_shape=(out, out, out), in_specs=[vmem] * 5, ou...  1.71 us

profile of v5, /device:TPU:1, one launch (start us, length us, event | category | flops | bytes accessed | tf_op | source)
XLA Modules:
  0.0 54.3 jit_solution(1670811639735654073)
XLA Ops:
  0.6 51.8 %shard_map.85 = (f32[32,32,256]{2,1,0:T(8,128)S(1)}, f32[32,32,256]{2,1,0:T(8,128)S(1)}, f32[40,2,48,128]{3,2,1,0:T(8,128)S(1)}, f32[40,2,48,128]{3,2,1,0:T(8,128)S(1)}, f32[40,2,48,128]{3,2,1,0:T(8,128)S(1)}) custom-call(f32[32,32,256]{2,1,0:T(8,128)} %conc_hbm.1, f32[32,32,256]{2,1,0:T(8,128)} %phi_hbm.1, f32[32,32,256]{2,1,0:T(8,128)} %solid_hbm.1, ...), custom_call_target="tpu_custom_call" | custom-call | tf_op jit(solution)/shard_map/pallas_call | solution.py:665
  52.4 1.7 %shard_map.86 = (f32[32,32,256]{2,1,0:T(8,128)}, f32[32,32,256]{2,1,0:T(8,128)}, f32[32,32,256]{2,1,0:T(8,128)}) custom-call(f32[32,32,256]{2,1,0:T(8,128)S(1)} %get-tuple-element.8.conc, f32[32,32,256]{2,1,0:T(8,128)S(1)} %get-tuple-element.9.flux, f32[40,2,48,128]{3,2,1,0:T(8,128)S(1)} %get-tuple-element.10.last, ...), custom_call_target="tpu_custom_call" | custom-call | tf_op jit(solution)/shard_map/pallas_call | solution.py:687
